TPU v7x, 256 devices: a whole 4x4x8 slice. The times are simulated.
256 devices in a mesh: rep: 32 (over z_hi, x, core), own: 8 (over z_lo, y).
Axes of the slice: x: 4, y: 4, z: 8 (z_hi: 4, z_lo: 2; z = z_hi * 2 + z_lo), core: 2. Of those that a mesh axis runs over, the one named last changes fastest.
Arguments:
- grads: bfloat16 [32, 8, 1024, 1024], P('rep', 'own'), may hold values from -4 to 4, as said below
- owners: int32 [8], replicated, may hold values from 0 to 7, as said below
- left_stats: float32 [8, 3, 1024, 1024], P('own', None, 'rep'), may hold values from -6 to 6
- right_stats: float32 [8, 3, 1024, 1024], P('own', None, 'rep'), may hold values from -6 to 6
- left_root: bfloat16 [8, 3, 1024, 1024], P('own', None, 'rep'), may hold values from -1 to 2
- right_root: bfloat16 [8, 3, 1024, 1024], P('own', None, 'rep'), may hold values from -1 to 2
- slot_weights: float32 [8, 3, 1024, 1024], P('own', None, 'rep'), may hold values from -6 to 6
- slot_second: float32 [8, 3, 1024, 1024], P('own', None, 'rep'), may hold values from 0.01 to 1
- norm_grads: bfloat16 [32, 8448], P('rep'), may hold values from -6 to 6
- norm_weights: float32 [8448], replicated, may hold values from 0.5 to 1.5
- norm_second: float32 [8448], replicated, may hold values from 0.01 to 1
Outputs:
- new_weights: float32 [8, 1024, 1024], P('own')
- new_left: float32 [8, 3, 1024, 1024], P('own', None, 'rep')
- new_right: float32 [8, 3, 1024, 1024], P('own', None, 'rep')
- new_second: float32 [8, 3, 1024, 1024], P('own', None, 'rep')
- new_norms: float32 [8448], replicated
- new_norm_second: float32 [8448], replicated
Inputs may be any that keep to these rules, and one draw needn't show every extreme that they name: `owners`: each owner holds at most 3 blocks, and some owner holds exactly 3. `grads`: every entry is a multiple of 1/64.
All inputs are finite; a program needn't handle non-finite values.
Results may differ from a plain program's by a relative error of at most 0.0054.
Values may be sent and summed in bfloat16 or wider, within the bound.
A program may use at most 128 MiB of HBM per device.

v0:
```python
import jax
import jax.numpy as jnp
from jax import lax
from jax.sharding import PartitionSpec as P

STAT_DECAY = 0.95
MOMENT_DECAY = 0.95
STEP_SIZE = 0.1
ADAM_EPS = 1e-08
GRAFT_EPS = 1e-06


def slot_numbers(owners):
    length = owners.shape[0]
    positions = jnp.arange(length, dtype=jnp.int32)
    same_owner = owners[:, None] == owners[None, :]
    before = positions[None, :] < positions[:, None]
    return jnp.sum((same_owner & before).astype(jnp.int32), axis=1)


def shards(
    grads,
    owners,
    left_stats,
    right_stats,
    left_root,
    right_root,
    slot_weights,
    slot_second,
    norm_grads,
    norm_weights,
    norm_second,
):
    own_here = lax.axis_index("own")
    rep_here = lax.axis_index("rep")
    blk_local = grads.shape[1]
    block_size = grads.shape[3]
    slot_count = left_stats.shape[1]
    row_count = left_stats.shape[2]
    slot_index = slot_numbers(owners)
    target = owners * slot_count + slot_index
    slot_range = jnp.arange(slot_count, dtype=jnp.int32)
    norm_sum = lax.psum(norm_grads[0].astype(jnp.float32), "rep")
    summed = lax.psum_scatter(grads[0].astype(jnp.float32), "rep", scatter_dimension=1, tiled=True)
    grad_held = summed.astype(jnp.bfloat16)
    shard_part = lax.all_gather(grad_held, "own", axis=0, tiled=True)
    wanted = (owners[None, :] == own_here) & (slot_index[None, :] == slot_range[:, None])
    owned_grad = jnp.einsum(
        "ki,irc->krc", wanted.astype(jnp.bfloat16), shard_part, preferred_element_type=jnp.float32
    ).astype(jnp.bfloat16)
    left_rows = left_root[0]
    shard_part = lax.all_gather(owned_grad, "rep", axis=1, tiled=True)
    products = jnp.einsum(
        "src,snc->srn", owned_grad, shard_part, preferred_element_type=jnp.float32
    )
    left_part = products
    mine_cols = lax.dynamic_slice_in_dim(shard_part, rep_here * row_count, row_count, 2)
    right_part = jnp.einsum(
        "snr,snc->src", mine_cols, shard_part, preferred_element_type=jnp.float32
    )
    accumulate_applied = jnp.einsum(
        "srn,snc->src", left_rows, shard_part, preferred_element_type=jnp.float32
    )
    left_part, right_part, applied = (left_part, right_part, accumulate_applied)
    shard_part = lax.all_gather(right_root[0], "rep", axis=1, tiled=True)
    direction = jnp.einsum(
        "srn,snc->src", applied, shard_part.astype(jnp.float32), precision=lax.Precision.HIGHEST
    )
    grad_f = owned_grad.astype(jnp.float32)
    new_second = MOMENT_DECAY * slot_second[0] + (1.0 - MOMENT_DECAY) * grad_f * grad_f
    adam_step = grad_f / (jnp.sqrt(new_second) + ADAM_EPS)
    adam_sq = jnp.sum(adam_step * adam_step, axis=(1, 2))
    dir_sq = jnp.sum(direction * direction, axis=(1, 2))
    adam_total, dir_total = lax.psum((adam_sq, dir_sq), "rep")
    cell_count = float(block_size * block_size)
    graft_scale = jnp.sqrt(adam_total / cell_count) / jnp.sqrt(dir_total / cell_count + GRAFT_EPS)
    updated = slot_weights[0] - STEP_SIZE * graft_scale[:, None, None] * direction
    mine_target = lax.dynamic_slice_in_dim(target, own_here * blk_local, blk_local)
    shard_part = lax.all_gather(updated, "own", axis=0, tiled=True)
    length = shard_part.shape[0]
    wanted = mine_target[:, None] == jnp.arange(length, dtype=jnp.int32)[None, :]
    held_rows = jnp.einsum(
        "ji,irc->jrc", wanted.astype(jnp.float32), shard_part, precision=lax.Precision.HIGHEST
    )
    new_weights = lax.all_gather(held_rows, "rep", axis=1, tiled=True)
    new_left = STAT_DECAY * left_stats[0] + (1.0 - STAT_DECAY) / block_size * left_part
    new_right = STAT_DECAY * right_stats[0] + (1.0 - STAT_DECAY) / block_size * right_part
    norm_moment = MOMENT_DECAY * norm_second + (1.0 - MOMENT_DECAY) * norm_sum * norm_sum
    new_norms = norm_weights - STEP_SIZE * norm_sum / (jnp.sqrt(norm_moment) + ADAM_EPS)
    return (new_weights, new_left[None], new_right[None], new_second[None], new_norms, norm_moment)


def solution(mesh):
    in_specs = (
        P("rep", "own", None, None),
        P(),
        P("own", None, "rep", None),
        P("own", None, "rep", None),
        P("own", None, "rep", None),
        P("own", None, "rep", None),
        P("own", None, "rep", None),
        P("own", None, "rep", None),
        P("rep", None),
        P(),
        P(),
    )
    out_specs = (
        P("own", None, None),
        P("own", None, "rep", None),
        P("own", None, "rep", None),
        P("own", None, "rep", None),
        P(),
        P(),
    )
    return jax.shard_map(shards, mesh=mesh, in_specs=in_specs, out_specs=out_specs, check_vma=False)
```

profile of v0, /device:TPU:1, one launch (start us, length us, event | category | flops | bytes accessed | tf_op | source)
XLA Modules:
  0.0 1193.3 jit_solution(12119739145021589492)
XLA Ops:
  7.2 0.0 copy-start
  7.2 0.0 all-gather.7.cloned.1.call-start
  7.2 0.9 convert_reduce_fusion.1
  8.2 0.7 broadcast_compare_fusion
  8.8 0.0 copy-start.9
  8.8 6.8 bitcast_convert_fusion
  15.7 0.0 copy-start.7
  15.7 0.0 copy-start.2
  15.7 736.7 %all-reduce.3 = bf16[1,1024,1024]{2,0,1:T(2,128)(2,1)} all-reduce(f32[1,1024,1024]{2,0,1:T(1,128)} %bitcast_convert_fusion), channel_id=4, replica_groups=mesh['rep'=32,'own'=8] {'rep'}, use_global_device_ids=true, to_apply=%region_1.0.clone | all-reduce | flops 1048576 | bytes 6291456
  752.4 0.0 copy-done.9
  752.4 0.6 dynamic-slice
  753.6 1.0 dynamic-slice_convert_fusion
  754.7 23.1 %all_gather.15 = bf16[8,32,1024]{2,1,0:T(8,128)(2,1)S(1)} all-gather(bf16[1,32,1024]{2,1,0:T(8,128)(2,1)S(1)} %copy.45), channel_id=1, replica_groups=mesh['rep'=32,'own'=8] {'own'}, dimensions={0}, use_global_device_ids=true | all-gather | bytes 589824 | tf_op jit(solution)/shard_map/all_gather | solution.py:46
  777.8 0.4 convolution_convert_fusion
  778.2 0.8 copy.48
  779.0 0.0 all-gather.7.cloned.1.call-update
  779.0 0.0 all-gather.11.cloned.1.call-start
  779.0 0.7 all-gather.11.cloned.1.call-update
  779.7 0.0 all-gather.9.cloned.1.call-start
  779.8 0.0 copy-done.7
  779.8 0.1 convert_reduce_fusion
  779.9 0.0 copy-done.2
  779.9 0.8 fusion.14
  780.7 0.0 copy-start.4
  780.7 0.0 copy-start.8
  780.7 73.9 %all-gather.7.cloned.1.call-done = bf16[3,1024,1024]{2,1,0:T(8,128)(2,1)} async-done(((bf16[3,32,1024]{2,1,0:T(8,128)(2,1)}), bf16[3,1024,1024]{2,1,0:T(8,128)(2,1)}) %all-gather.7.cloned.1.call-update) | async-done | bytes 6291472 | tf_op jit(solution)/shard_map/all_gather | solution.py:52
  854.7 0.0 copy-done
  854.7 4.0 fusion.15
  858.6 0.0 copy-start.3
  858.6 65.7 %all-gather.11.cloned.1.call-done = bf16[1,3,1024,1024]{3,2,1,0:T(8,128)(2,1)} async-done(((bf16[1,3,32,1024]{3,2,1,0:T(8,128)(2,1)}), bf16[1,3,1024,1024]{3,2,1,0:T(8,128)(2,1)}) %all-gather.11.cloned.1.call-update) | async-done | bytes 6291472 | tf_op jit(solution)/shard_map/all_gather | solution.py:65
  924.3 5.3 multiply_reduce_fusion
  929.6 136.1 %all-reduce.1 = (f32[3]{0:T(128)S(1)}, f32[3]{0:T(128)S(1)}, f32[8448]{0:T(1024)S(1)}) all-reduce(f32[3]{0:T(128)S(1)} %get-tuple-element.31, f32[3]{0:T(128)S(1)} %get-tuple-element.30, f32[8448]{0:T(1024)S(1)} %convert_reduce_fusion), channel_id=1, replica_groups=mesh['rep'=32,'own'=8] {'rep'}, use_global_device_ids=true, to_apply=%region_5.0 | all-reduce | flops 8454 | bytes 67632 | tf_op jit(solution)/shard_map/psum | solution.py:74
  1065.8 0.0 copy-done.4
  1065.8 0.9 bitcast_subtract_fusion
  1066.6 0.0 all-gather.9.cloned.1.call-update
  1066.7 0.2 all-gather.13.cloned.1.call-start
  1066.9 0.0 copy-done.8
  1066.9 0.6 dynamic_slice.6
  1067.5 45.5 %all-gather.9.cloned.1.call-done = f32[24,32,1024]{2,1,0:T(8,128)} async-done(((f32[3,32,1024]{2,1,0:T(8,128)}), f32[24,32,1024]{2,1,0:T(8,128)}) %all-gather.9.cloned.1.call-update) | async-done | bytes 3145744 | tf_op jit(solution)/shard_map/all_gather | solution.py:79
  1113.0 5.3 fusion.2
  1118.3 0.0 slice-start
  1118.3 0.0 copy-start.1
  1118.4 0.7 copy.93
  1119.0 0.0 all-gather.13.cloned.1.call-update
  1119.1 1.0 copy.57
  1120.0 0.0 copy-done.3
  1120.1 1.0 broadcast_multiply_fusion.1
  1121.1 0.0 slice-start.1
  1121.1 4.7 fusion.4
  1125.8 0.0 copy-start.5
  1125.8 0.0 copy-start.6
  1125.9 0.5 fusion.9
  1126.4 1.0 copy.56
  1127.4 0.0 slice-done
  1127.4 0.0 copy-done.1
  1127.4 0.0 slice-done.1
  1127.4 1.9 fusion.30
  1129.3 0.6 fusion.11
  1129.9 1.0 copy.55
  1130.9 0.0 copy-done.5
  1130.9 0.0 copy-done.6
  1130.9 0.7 divide_subtract_fusion
  1131.5 50.4 %all-gather.13.cloned.1.call-done = f32[1024,1024]{1,0:T(8,128)} async-done(((f32[32,1024]{1,0:T(8,128)}), f32[1024,1024]{1,0:T(8,128)}) %all-gather.13.cloned.1.call-update) | async-done | bytes 4194320 | tf_op jit(solution)/shard_map/all_gather | solution.py:85
  1182.0 4.8 copy.97
  (6 shorter events, 0.1 us)
Async XLA Ops:
  7.2 847.5 %copy-start = (bf16[1,3,32,1024]{3,2,1,0:T(8,128)(2,1)S(1)}, bf16[1,3,32,1024]{3,2,1,0:T(8,128)(2,1)}, u32[]{:S(2)}) copy-start(bf16[1,3,32,1024]{3,2,1,0:T(8,128)(2,1)} %param.15) | copy-start | bytes 589828
  7.2 847.5 %all-gather.7.cloned.1.call-start = ((), (), s32[]{:S(2)}) async-start(), calls=%async_computation | async-start | bytes 6488064 | tf_op jit(solution)/shard_map/all_gather | solution.py:52
  8.8 743.6 %copy-start.9 = (u32[256]{0:T(256)S(1)}, u32[256]{0:T(256)}, u32[]{:S(2)}) copy-start(u32[256]{0:T(256)} %constant.51) | copy-start | bytes 3076
  15.7 764.1 %copy-start.7 = (bf16[1,8448]{1,0:T(2,128)(2,1)S(1)}, bf16[1,8448]{1,0:T(2,128)(2,1)}, u32[]{:S(2)}) copy-start(bf16[1,8448]{1,0:T(2,128)(2,1)} %param.19) | copy-start | bytes 50692
  15.7 764.2 %copy-start.2 = (f32[1,3,32,1024]{3,2,1,0:T(8,128)S(1)}, f32[1,3,32,1024]{3,2,1,0:T(8,128)}, u32[]{:S(2)}) copy-start(f32[1,3,32,1024]{3,2,1,0:T(8,128)} %param.18) | copy-start | bytes 1179652
  779.0 145.4 %all-gather.11.cloned.1.call-start = ((), (), s32[]{:S(2)}) async-start(), calls=%async_computation.2 | async-start | bytes 6488064 | tf_op jit(solution)/shard_map/all_gather | solution.py:65
  779.7 333.2 %all-gather.9.cloned.1.call-start = ((), (), s32[]{:S(2)}) async-start(), calls=%async_computation.1 | async-start | bytes 3538944 | tf_op jit(solution)/shard_map/all_gather | solution.py:79
  780.7 285.1 %copy-start.4 = (f32[1,3,32,1024]{3,2,1,0:T(8,128)S(1)}, f32[1,3,32,1024]{3,2,1,0:T(8,128)}, u32[]{:S(2)}) copy-start(f32[1,3,32,1024]{3,2,1,0:T(8,128)} %param.17) | copy-start | bytes 1179652
  780.7 286.2 %copy-start.8 = (s32[8]{0:T(128)S(1)}, s32[8]{0:T(128)}, u32[]{:S(2)}) copy-start(s32[8]{0:T(128)} %param.12) | copy-start | bytes 100
  858.6 261.4 %copy-start.3 = (f32[1,3,32,1024]{3,2,1,0:T(8,128)S(1)}, f32[1,3,32,1024]{3,2,1,0:T(8,128)}, u32[]{:S(2)}) copy-start(f32[1,3,32,1024]{3,2,1,0:T(8,128)} %param.14) | copy-start | bytes 1179652
  1066.7 115.3 %all-gather.13.cloned.1.call-start = ((), (), s32[]{:S(2)}) async-start(), calls=%async_computation.3 | async-start | bytes 4325376 | tf_op jit(solution)/shard_map/all_gather | solution.py:85
  1118.3 9.1 slice-start
  1118.3 9.1 copy-start.1
  1121.1 6.3 slice-start.1
  1125.8 5.1 copy-start.5
  1125.8 5.0 copy-start.6
Sparse Core Ops, SparseCore 0:
  779.1 75.5 all-gather.6
  857.3 67.0 all-gather.10
  1066.8 46.1 all-gather.8
  1119.2 62.7 all-gather.12
where the time goes:
time: 1190 us
  blocking collectives  896 us (75%)
  waiting for transfers between devices  236 us (20%)
  matrix products  21.7 us (2%)
  between operations  14.6 us (1%)
  other arithmetic  13 us (1%)
    unnamed x1, blocking collectives  737 us
    psum x1, blocking collectives, shards(): adam_total, dir_total = lax.psum((adam_sq, dir_sq), 'rep')  136 us
    all_gather x1, waiting for transfers between devices, shards(): shard_part = lax.all_gather(owned_grad, 'rep', axis=1, tiled=True)  73.9 us
    all_gather x1, waiting for transfers between devices, shards(): shard_part = lax.all_gather(right_root[0], 'rep', axis=1, tiled=True)  65.7 us
    all_gather x1, waiting for transfers between devices, shards(): new_weights = lax.all_gather(held_rows, 'rep', axis=1, tiled=True)  50.4 us
    all_gather x1, waiting for transfers between devices, shards(): shard_part = lax.all_gather(updated, 'own', axis=0, tiled=True)  45.5 us
  transfers between devices with their start and end apart: 4, of which 4 were waited for; matrix products, arithmetic and copies ran while one was open for 1% of the time, Pallas kernels for 0%

commit v1 on v0

--- a/solution.py
+++ b/solution.py
@@ -40,9 +40,12 @@
     slot_index = slot_numbers(owners)
     target = owners * slot_count + slot_index
     slot_range = jnp.arange(slot_count, dtype=jnp.int32)
-    norm_sum = lax.psum(norm_grads[0].astype(jnp.float32), "rep")
-    summed = lax.psum_scatter(grads[0].astype(jnp.float32), "rep", scatter_dimension=1, tiled=True)
-    grad_held = summed.astype(jnp.bfloat16)
+    rep_count = block_size // row_count
+    norm_all = lax.all_gather(norm_grads[0], "rep", axis=0, tiled=False)
+    norm_sum = jnp.sum(norm_all.astype(jnp.float32), axis=0)
+    grad_rows = grads[0, 0].astype(jnp.float32).reshape(rep_count, row_count, block_size)
+    summed = lax.psum_scatter(grad_rows, "rep", scatter_dimension=0, tiled=False)
+    grad_held = lax.optimization_barrier(summed).astype(jnp.bfloat16)[None]
     shard_part = lax.all_gather(grad_held, "own", axis=0, tiled=True)
     wanted = (owners[None, :] == own_here) & (slot_index[None, :] == slot_range[:, None])
     owned_grad = jnp.einsum(
@@ -71,7 +74,8 @@
     adam_step = grad_f / (jnp.sqrt(new_second) + ADAM_EPS)
     adam_sq = jnp.sum(adam_step * adam_step, axis=(1, 2))
     dir_sq = jnp.sum(direction * direction, axis=(1, 2))
-    adam_total, dir_total = lax.psum((adam_sq, dir_sq), "rep")
+    sq_all = lax.all_gather(jnp.stack([adam_sq, dir_sq]), "rep", axis=0, tiled=False)
+    adam_total, dir_total = jnp.sum(sq_all, axis=0)
     cell_count = float(block_size * block_size)
     graft_scale = jnp.sqrt(adam_total / cell_count) / jnp.sqrt(dir_total / cell_count + GRAFT_EPS)
     updated = slot_weights[0] - STEP_SIZE * graft_scale[:, None, None] * direction

time: 1190 us -> 459 us (0.39)
  blocking collectives: 896 us -> 121 us
  waiting for transfers between devices: 236 us -> 281 us
    unnamed x1 -> x0, blocking collectives: 737 us -> none
    psum x1 -> x0, blocking collectives: 136 us -> none  [shards(): adam_total, dir_total = lax.psum((adam_sq, dir_sq), 'rep')]
    reduce_scatter x0 -> x1, waiting for transfers between devices: none -> 102 us  [shards(): lax.psum_scatter(grad_rows, 'rep', scatter_dimension=0, tiled=False)]
    all_gather x0 -> x2, blocking collectives: none -> 98.1 us  [the longest x1 54.6 us: shards(): norm_all = lax.all_gather(norm_grads[0], 'rep', axis=0, tiled=False)]
    all_gather x1, waiting for transfers between devices: 50.4 us -> 0.01 us  [shards(): new_weights = lax.all_gather(held_rows, 'rep', axis=1, tiled=True)]
  transfers between devices with their start and end apart: 4 -> 5, of which waited for: 4 -> 4; matrix products, arithmetic and copies ran while one was open for 1% -> 4% of each run, Pallas kernels for 0% -> 0%
where the time goes in v1:
time: 459 us; the launch traced here: 458 us
  waiting for transfers between devices  281 us (61%)
  blocking collectives  121 us (26%)
  matrix products  21.4 us (5%)
  between operations  14 us (3%)
  other arithmetic  10 us (2%)
  local copies, waits for them, and re-layouts  9.81 us (2%)
    reduce_scatter x1, waiting for transfers between devices, shards(): lax.psum_scatter(grad_rows, 'rep', scatter_dimension=0, tiled=False)  102 us
    all_gather x1, waiting for transfers between devices, shards(): shard_part = lax.all_gather(owned_grad, 'rep', axis=1, tiled=True)  73 us
    all_gather x1, waiting for transfers between devices, shards(): shard_part = lax.all_gather(right_root[0], 'rep', axis=1, tiled=True)  65.7 us
    all_gather x1, blocking collectives, shards(): norm_all = lax.all_gather(norm_grads[0], 'rep', axis=0, tiled=False)  54.6 us
    all_gather x1, blocking collectives, shards(): lax.all_gather(jnp.stack([adam_sq, dir_sq]), 'rep', axis=0, tiled=False)  43.5 us
    all_gather x1, waiting for transfers between devices, shards(): shard_part = lax.all_gather(updated, 'own', axis=0, tiled=True)  39.3 us
    all_gather x1, blocking collectives, shards(): shard_part = lax.all_gather(grad_held, 'own', axis=0, tiled=True)  23 us
  transfers between devices with their start and end apart: 5, of which 4 were waited for; matrix products, arithmetic and copies ran while one was open for 4% of the time, Pallas kernels for 0%

profile of v1, /device:TPU:1, one launch (start us, length us, event | category | flops | bytes accessed | tf_op | source)
XLA Modules:
  0.0 457.6 jit_solution(11593402862658850500)
XLA Ops:
  7.2 0.0 copy-start
  7.2 0.0 copy-start.9
  7.2 0.0 reduce-scatter.2.cloned.1.call-start
  7.2 0.0 copy-start.2
  7.2 4.1 convert.1
  11.4 0.0 reduce-scatter.2.cloned.1.call-update
  11.4 0.0 all-gather.11.cloned.1.call-start
  11.5 0.0 copy-done.9
  11.5 0.2 convert_reduce_fusion.1
  11.7 102.3 %reduce-scatter.2.cloned.1.call-done = f32[1,32,1024]{2,1,0:T(8,128)} async-done(((f32[32,32,1024]{2,1,0:T(8,128)}), f32[1,32,1024]{2,1,0:T(8,128)}) %reduce-scatter.2.cloned.1.call-update) | async-done | bytes 131088 | tf_op jit(solution)/shard_map/reduce_scatter | solution.py:47
  114.0 0.9 convert_element_type.28
  114.9 23.0 %all-gather = bf16[256,1024]{1,0:T(8,128)(2,1)S(1)} all-gather(bf16[32,1024]{1,0:T(8,128)(2,1)S(1)} %convert_element_type.28), channel_id=2, replica_groups=mesh['rep'=32,'own'=8] {'own'}, dimensions={0}, use_global_device_ids=true | all-gather | bytes 589824 | tf_op jit(solution)/shard_map/all_gather | solution.py:49
  137.9 0.4 convolution_convert_fusion
  138.3 0.8 copy.56
  139.0 0.0 all-gather.11.cloned.1.call-update
  139.1 0.0 all-gather.15.cloned.1.call-start
  139.1 0.7 all-gather.15.cloned.1.call-update
  139.8 0.0 all-gather.13.cloned.1.call-start
  139.8 0.0 copy-done.2
  139.9 0.8 fusion.14
  140.7 0.0 copy-start.5
  140.7 73.0 %all-gather.11.cloned.1.call-done = bf16[3,1024,1024]{2,1,0:T(8,128)(2,1)} async-done(((bf16[3,32,1024]{2,1,0:T(8,128)(2,1)}), bf16[3,1024,1024]{2,1,0:T(8,128)(2,1)}) %all-gather.11.cloned.1.call-update) | async-done | bytes 6291472 | tf_op jit(solution)/shard_map/all_gather | solution.py:55
  213.7 0.0 copy-done
  213.7 4.0 fusion.15
  217.7 0.0 copy-start.8
  217.7 0.0 copy-start.3
  217.7 0.0 copy-start.4
  217.7 65.7 %all-gather.15.cloned.1.call-done = bf16[1,3,1024,1024]{3,2,1,0:T(8,128)(2,1)} async-done(((bf16[1,3,32,1024]{3,2,1,0:T(8,128)(2,1)}), bf16[1,3,1024,1024]{3,2,1,0:T(8,128)(2,1)}) %all-gather.15.cloned.1.call-update) | async-done | bytes 6291472 | tf_op jit(solution)/shard_map/all_gather | solution.py:68
  283.4 5.3 %multiply_reduce_fusion = (f32[3]{0:T(128)S(1)}, f32[3,32,1024]{2,1,0:T(8,128)S(1)}) fusion(f32[3,1024,32]{1,2,0:T(8,128)S(1)} %fusion.15, bf16[1,3,1024,1024]{3,2,1,0:T(8,128)(2,1)} %all-gather.15.cloned.1.call-done), kind=kOutput, calls=%fused_computation.24 | convolution fusion | flops 1208156160 | bytes 7077900 | tf_op jit(solution)/shard_map/srn,snc->src/dot_general | solution.py:69
  288.7 0.0 copy-start.6
  288.7 0.0 copy-start.7
  288.7 0.0 copy-start.1
  288.7 43.5 %all-gather.4 = f32[32,2,3]{2,1,0:T(2,128)S(1)} all-gather(f32[1,2,3]{2,1,0:T(2,128)S(1)} %maximum_bitcast_fusion), channel_id=4, replica_groups=mesh['rep'=32,'own'=8] {'rep'}, dimensions={0}, use_global_device_ids=true | all-gather | bytes 792 | tf_op jit(solution)/shard_map/all_gather | solution.py:77
  332.3 0.0 copy-done.5
  332.3 0.9 bitcast_subtract_fusion
  333.1 0.0 all-gather.13.cloned.1.call-update
  333.1 0.0 all-gather.17.cloned.1.call-start
  333.2 0.6 dynamic_slice.6
  333.8 39.3 %all-gather.13.cloned.1.call-done = f32[24,32,1024]{2,1,0:T(8,128)} async-done(((f32[3,32,1024]{2,1,0:T(8,128)}), f32[24,32,1024]{2,1,0:T(8,128)}) %all-gather.13.cloned.1.call-update) | async-done | bytes 3145744 | tf_op jit(solution)/shard_map/all_gather | solution.py:83
  373.1 5.3 %fusion.2 = f32[1,32,1024]{2,0,1:T(1,128)S(1)} fusion(f32[24,32,1024]{2,1,0:T(8,128)} %all-gather.13.cloned.1.call-done, s32[]{:T(128)} %bitcast), kind=kOutput, calls=%fused_computation.2 | convolution fusion | flops 9437208 | bytes 3276804 | tf_op jit(solution)/shard_map/ji,irc->jrc/dot_general | solution.py:86
  378.4 0.7 copy.100
  379.1 0.0 all-gather.17.cloned.1.call-update
  379.1 0.0 copy-done.8
  379.1 54.6 %all-gather.5 = bf16[32,1,8448]{2,1,0:T(2,128)(2,1)S(1)} all-gather(bf16[1,1,8448]{2,1,0:T(2,128)(2,1)S(1)} %bitcast.70), channel_id=1, replica_groups=mesh['rep'=32,'own'=8] {'rep'}, dimensions={0}, use_global_device_ids=true | all-gather | bytes 557568 | tf_op jit(solution)/shard_map/all_gather | solution.py:44
  433.8 0.0 slice-start
  433.8 1.2 convert_reduce_fusion
  435.0 0.0 copy-done.3
  435.0 0.0 copy-done.4
  435.1 0.0 copy-done.6
  435.1 0.0 copy-done.7
  435.1 0.7 divide_subtract_fusion
  435.8 1.0 copy.65
  436.7 0.0 copy-done.1
  436.7 0.0 slice-start.1
  436.7 4.9 %fusion.30 = f32[3,32,1024]{2,1,0:T(8,128)S(1)} fusion(bf16[3,32,1024]{2,1,0:T(8,128)(2,1)S(1)} %copy-done.1, bf16[3,1024,1024]{2,1,0:T(8,128)(2,1)} %all-gather.11.cloned.1.call-done), kind=kOutput, calls=%fused_computation.52 | convolution fusion | flops 201326592 | bytes 6881280 | tf_op jit(solution)/shard_map/src,snc->srn/dot_general | solution.py:56
  441.7 0.6 fusion.11
  442.2 1.0 copy.63
  443.2 0.0 slice-done
  443.2 0.0 slice-done.1
  443.2 1.5 fusion.4
  444.7 0.5 fusion.9
  445.3 1.0 copy.64
  446.3 0.0 all-gather.17.cloned.1.call-done
  446.3 4.8 %copy.102 = f32[1,1024,1024]{2,1,0:T(8,128)} copy(f32[1,1024,1024]{2,1,0:T(8,128)} %bitcast.65) | data formatting | bytes 8388608
  (9 shorter events, 0.2 us)
Async XLA Ops:
  7.2 206.6 %copy-start = (bf16[1,3,32,1024]{3,2,1,0:T(8,128)(2,1)S(1)}, bf16[1,3,32,1024]{3,2,1,0:T(8,128)(2,1)}, u32[]{:S(2)}) copy-start(bf16[1,3,32,1024]{3,2,1,0:T(8,128)(2,1)} %param.15) | copy-start | bytes 589828
  7.2 4.3 copy-start.9
  7.2 106.8 %reduce-scatter.2.cloned.1.call-start = ((), (), s32[]{:S(2)}) async-start(), calls=%async_computation.1 | async-start | bytes 4325376 | tf_op jit(solution)/shard_map/reduce_scatter | solution.py:47
  7.2 132.6 %copy-start.2 = (f32[1,3,32,1024]{3,2,1,0:T(8,128)S(1)}, f32[1,3,32,1024]{3,2,1,0:T(8,128)}, u32[]{:S(2)}) copy-start(f32[1,3,32,1024]{3,2,1,0:T(8,128)} %param.18) | copy-start | bytes 1179652
  11.4 202.3 %all-gather.11.cloned.1.call-start = ((), (), s32[]{:S(2)}) async-start(), calls=%async_computation.2 | async-start | bytes 6488064 | tf_op jit(solution)/shard_map/all_gather | solution.py:55
  139.1 144.3 %all-gather.15.cloned.1.call-start = ((), (), s32[]{:S(2)}) async-start(), calls=%async_computation.4 | async-start | bytes 6488064 | tf_op jit(solution)/shard_map/all_gather | solution.py:68
  139.8 233.3 %all-gather.13.cloned.1.call-start = ((), (), s32[]{:S(2)}) async-start(), calls=%async_computation.3 | async-start | bytes 3538944 | tf_op jit(solution)/shard_map/all_gather | solution.py:83
  140.7 191.6 %copy-start.5 = (f32[1,3,32,1024]{3,2,1,0:T(8,128)S(1)}, f32[1,3,32,1024]{3,2,1,0:T(8,128)}, u32[]{:S(2)}) copy-start(f32[1,3,32,1024]{3,2,1,0:T(8,128)} %param.17) | copy-start | bytes 1179652
  217.7 161.4 %copy-start.8 = (bf16[1,8448]{1,0:T(2,128)(2,1)S(1)}, bf16[1,8448]{1,0:T(2,128)(2,1)}, u32[]{:S(2)}) copy-start(bf16[1,8448]{1,0:T(2,128)(2,1)} %param.19) | copy-start | bytes 50692
  217.7 217.3 %copy-start.3 = (f32[1,3,32,1024]{3,2,1,0:T(8,128)S(1)}, f32[1,3,32,1024]{3,2,1,0:T(8,128)}, u32[]{:S(2)}) copy-start(f32[1,3,32,1024]{3,2,1,0:T(8,128)} %param.13) | copy-start | bytes 1179652
  217.7 217.3 %copy-start.4 = (f32[1,3,32,1024]{3,2,1,0:T(8,128)S(1)}, f32[1,3,32,1024]{3,2,1,0:T(8,128)}, u32[]{:S(2)}) copy-start(f32[1,3,32,1024]{3,2,1,0:T(8,128)} %param.14) | copy-start | bytes 1179652
  288.7 146.4 %copy-start.6 = (f32[8448]{0:T(1024)S(1)}, f32[8448]{0:T(1024)}, u32[]{:S(2)}) copy-start(f32[8448]{0:T(1024)} %param.20) | copy-start | bytes 101380
  288.7 146.4 %copy-start.7 = (f32[8448]{0:T(1024)S(1)}, f32[8448]{0:T(1024)}, u32[]{:S(2)}) copy-start(f32[8448]{0:T(1024)} %param.21) | copy-start | bytes 101380
  288.7 148.0 %copy-start.1 = (bf16[3,32,1024]{2,1,0:T(8,128)(2,1)S(1)}, bf16[3,32,1024]{2,1,0:T(8,128)(2,1)}, u32[]{:S(2)}) copy-start(bf16[3,32,1024]{2,1,0:T(8,128)(2,1)} %copy.56) | copy-start | bytes 589828
  333.1 113.1 %all-gather.17.cloned.1.call-start = ((), (), s32[]{:S(2)}) async-start(), calls=%async_computation.5 | async-start | bytes 4325376 | tf_op jit(solution)/shard_map/all_gather | solution.py:89
  433.8 9.4 %slice-start = ((s8[6291456]{0:T(1024)(128)(4,1)}), s8[4194304]{0:T(1024)(128)(4,1)S(1)}, s32[]{:S(2)}) async-start(s8[6291456]{0:T(1024)(128)(4,1)} %bitcast.63), calls=%async_computation.6 | async-start | bytes 8388608
  436.7 6.5 %slice-start.1 = ((s8[6291456]{0:T(1024)(128)(4,1)}), s8[2097152]{0:T(1024)(128)(4,1)S(1)}, s32[]{:S(2)}) async-start(s8[6291456]{0:T(1024)(128)(4,1)} %bitcast.63), calls=%async_computation.7 | async-start | bytes 4194304
Sparse Core Ops, SparseCore 0:
  12.5 101.4 reduce-scatter.1
  139.2 74.4 all-gather.10
  216.3 67.0 all-gather.14
  333.3 39.7 all-gather.12
  379.2 63.3 all-gather.16

commit v2 on v1

--- a/solution.py
+++ b/solution.py
@@ -16,6 +16,26 @@
     same_owner = owners[:, None] == owners[None, :]
     before = positions[None, :] < positions[:, None]
     return jnp.sum((same_owner & before).astype(jnp.int32), axis=1)
+
+
+def rep_gather(value, rep_count):
+    rep_here = lax.axis_index("rep")
+    sizes = (rep_count // 8, 4, 2)
+    strides = (8, 2, 1)
+    bundle = value[None]
+    for size, stride in zip(sizes, strides):
+        coord = (rep_here // stride) % size
+        parts = [bundle]
+        for shift in range(1, size):
+            pairs = []
+            for j in range(rep_count):
+                u = (j // stride) % size
+                pairs.append((j, j + ((u + shift) % size - u) * stride))
+            parts.append(lax.ppermute(bundle, "rep", pairs))
+        stacked = jnp.stack(parts)
+        order = (coord - jnp.arange(size, dtype=jnp.int32)) % size
+        bundle = jnp.take(stacked, order, axis=0).reshape((size * bundle.shape[0],) + bundle.shape[1:])
+    return bundle.reshape((2, 4, rep_count // 8) + value.shape)
 
 
 def shards(
@@ -41,8 +61,9 @@
     target = owners * slot_count + slot_index
     slot_range = jnp.arange(slot_count, dtype=jnp.int32)
     rep_count = block_size // row_count
-    norm_all = lax.all_gather(norm_grads[0], "rep", axis=0, tiled=False)
-    norm_sum = jnp.sum(norm_all.astype(jnp.float32), axis=0)
+    norm_all = rep_gather(norm_grads[0], rep_count)
+    norm_sum = jnp.sum(norm_all.astype(jnp.float32), axis=(0, 1, 2))
+    right_all = rep_gather(right_root[0], rep_count)
     grad_rows = grads[0, 0].astype(jnp.float32).reshape(rep_count, row_count, block_size)
     summed = lax.psum_scatter(grad_rows, "rep", scatter_dimension=0, tiled=False)
     grad_held = lax.optimization_barrier(summed).astype(jnp.bfloat16)[None]
@@ -65,17 +86,17 @@
         "srn,snc->src", left_rows, shard_part, preferred_element_type=jnp.float32
     )
     left_part, right_part, applied = (left_part, right_part, accumulate_applied)
-    shard_part = lax.all_gather(right_root[0], "rep", axis=1, tiled=True)
+    applied_parts = applied.reshape(applied.shape[:2] + (rep_count // 8, 4, 2, row_count))
     direction = jnp.einsum(
-        "srn,snc->src", applied, shard_part.astype(jnp.float32), precision=lax.Precision.HIGHEST
+        "smzxcr,cxzsrk->smk", applied_parts, right_all.astype(jnp.float32), precision=lax.Precision.HIGHEST
     )
     grad_f = owned_grad.astype(jnp.float32)
     new_second = MOMENT_DECAY * slot_second[0] + (1.0 - MOMENT_DECAY) * grad_f * grad_f
     adam_step = grad_f / (jnp.sqrt(new_second) + ADAM_EPS)
     adam_sq = jnp.sum(adam_step * adam_step, axis=(1, 2))
     dir_sq = jnp.sum(direction * direction, axis=(1, 2))
-    sq_all = lax.all_gather(jnp.stack([adam_sq, dir_sq]), "rep", axis=0, tiled=False)
-    adam_total, dir_total = jnp.sum(sq_all, axis=0)
+    sq_all = rep_gather(jnp.stack([adam_sq, dir_sq]), rep_count)
+    adam_total, dir_total = jnp.sum(sq_all, axis=(0, 1, 2))
     cell_count = float(block_size * block_size)
     graft_scale = jnp.sqrt(adam_total / cell_count) / jnp.sqrt(dir_total / cell_count + GRAFT_EPS)
     updated = slot_weights[0] - STEP_SIZE * graft_scale[:, None, None] * direction

time: 459 us -> 399 us (0.87)
  blocking collectives: 121 us -> 23 us
  waiting for transfers between devices: 281 us -> 240 us
  starting transfers between devices: 0.2 us -> 37.9 us
  local copies, waits for them, and re-layouts: 9.81 us -> 32 us
  other arithmetic: 10 us -> 27.4 us
    all_gather x2 -> x0, blocking collectives: 98.1 us -> none  [the longest x1 54.6 us: shards(): norm_all = lax.all_gather(norm_grads[0], 'rep', axis=0, tiled=False)]
    all_gather x1, waiting for transfers between devices: 73 us -> 0.01 us  [shards(): shard_part = lax.all_gather(owned_grad, 'rep', axis=1, tiled=True)]
    all_gather x1 -> x0, waiting for transfers between devices: 65.7 us -> none  [shards(): shard_part = lax.all_gather(right_root[0], 'rep', axis=1, tiled=True)]
    ppermute x0 -> x21, waiting for transfers between devices: none -> 65.5 us  [rep_gather(): parts.append(lax.ppermute(bundle, 'rep', pairs))]
    all_gather x1, waiting for transfers between devices: 0.01 us -> 43.9 us  [shards(): new_weights = lax.all_gather(held_rows, 'rep', axis=1, tiled=True)]
    ppermute x0 -> x21, starting transfers between devices: none -> 37.8 us  [rep_gather(): parts.append(lax.ppermute(bundle, 'rep', pairs))]
    gather x0 -> x16, local copies, waits for them, and re-layouts: none -> 14.1 us  [rep_gather(): jnp.take(stacked, order, axis=0)]
    all_gather x1, waiting for transfers between devices: 39.3 us -> 28.6 us  [shards(): shard_part = lax.all_gather(updated, 'own', axis=0, tiled=True)]
  transfers between devices with their start and end apart: 5 -> 25, of which waited for: 4 -> 16; matrix products, arithmetic and copies ran while one was open for 4% -> 14% of each run, Pallas kernels for 0% -> 0%
where the time goes in v2:
time: 399 us
  waiting for transfers between devices  240 us (60%)
  starting transfers between devices  37.9 us (9%)
  local copies, waits for them, and re-layouts  32 us (8%)
  other arithmetic  27.4 us (7%)
  matrix products  24.4 us (6%)
  blocking collectives  23 us (6%)
  between operations  14.2 us (4%)
    reduce_scatter x1, waiting for transfers between devices, shards(): lax.psum_scatter(grad_rows, 'rep', scatter_dimension=0, tiled=False)  102 us
    ppermute x21, waiting for transfers between devices, rep_gather(): parts.append(lax.ppermute(bundle, 'rep', pairs))  65.5 us
    all_gather x1, waiting for transfers between devices, shards(): new_weights = lax.all_gather(held_rows, 'rep', axis=1, tiled=True)  43.9 us
    ppermute x21, starting transfers between devices, rep_gather(): parts.append(lax.ppermute(bundle, 'rep', pairs))  37.8 us
    all_gather x1, waiting for transfers between devices, shards(): shard_part = lax.all_gather(updated, 'own', axis=0, tiled=True)  28.6 us
    all_gather x1, blocking collectives, shards(): shard_part = lax.all_gather(grad_held, 'own', axis=0, tiled=True)  23 us
    gather x16, local copies, waits for them, and re-layouts, rep_gather(): jnp.take(stacked, order, axis=0)  14.1 us
    unnamed x37, local copies, waits for them, and re-layouts  14.1 us
  transfers between devices with their start and end apart: 25, of which 16 were waited for; matrix products, arithmetic and copies ran while one was open for 14% of the time, Pallas kernels for 0%

profile of v2, /device:TPU:1, one launch (start us, length us, event | category | flops | bytes accessed | tf_op | source)
XLA Modules:
  0.0 398.6 jit_solution(5136941563382932813)
XLA Ops:
  7.2 4.1 %convert.1 = f32[32,32,1024]{2,1,0:T(8,128)} convert(bf16[32,32,1024]{2,1,0:T(8,128)(2,1)} %bitcast.118) | non-fusion elementwise | flops 1048576 | bytes 6291456 | tf_op jit(solution)/shard_map/convert_element_type | solution.py:67
  12.2 101.8 %reduce-scatter.2.cloned.1.call-done = f32[1,32,1024]{2,1,0:T(8,128)} async-done(((f32[32,32,1024]{2,1,0:T(8,128)}), f32[1,32,1024]{2,1,0:T(8,128)}) %reduce-scatter.2.cloned.1.call-update) | async-done | bytes 131088 | tf_op jit(solution)/shard_map/reduce_scatter | solution.py:68
  114.0 0.9 convert_element_type.29
  114.9 23.0 %all-gather = bf16[256,1024]{1,0:T(8,128)(2,1)S(1)} all-gather(bf16[32,1024]{1,0:T(8,128)(2,1)S(1)} %convert_element_type.29), channel_id=2, replica_groups=mesh['rep'=32,'own'=8] {'own'}, dimensions={0}, use_global_device_ids=true | all-gather | bytes 589824 | tf_op jit(solution)/shard_map/all_gather | solution.py:70
  138.3 0.7 copy-done.1
  139.0 0.8 copy.105
  139.8 1.7 collective-permute-start
  141.6 1.9 collective-permute-start.2
  143.5 3.8 collective-permute-start.1
  147.3 1.5 collective-permute-done
  148.7 1.6 collective-permute-done.2
  150.4 4.9 %collective-permute-done.1 = bf16[1,3,32,1024]{3,2,1,0:T(8,128)(2,1)S(1)} collective-permute-done((bf16[1,3,32,1024]{3,2,1,0:T(8,128)(2,1)S(1)}, bf16[1,3,32,1024]{3,2,1,0:T(8,128)(2,1)S(1)}, u32[]{:S(2)}, u32[]{:S(2)}) %collective-permute-start.1) | collective-permute-done | bytes 196640 | tf_op jit(solution)/shard_map/ppermute | solution.py:34
  155.4 0.6 gather_fusion
  156.0 1.0 broadcast_select_fusion
  157.0 1.5 collective-permute-start.3
  158.8 12.0 %collective-permute-done.5 = bf16[4,3,32,1024]{3,2,1,0:T(8,128)(2,1)S(1)} collective-permute-done((bf16[4,3,32,1024]{3,2,1,0:T(8,128)(2,1)}, bf16[4,3,32,1024]{3,2,1,0:T(8,128)(2,1)S(1)}, u32[]{:S(2)}, u32[]{:S(2)}) %collective-permute-start.5) | collective-permute-done | bytes 786464 | tf_op jit(solution)/shard_map/ppermute | solution.py:34
  171.3 30.2 %collective-permute-done.3 = bf16[4,3,32,1024]{3,2,1,0:T(8,128)(2,1)S(1)} collective-permute-done((bf16[4,3,32,1024]{3,2,1,0:T(8,128)(2,1)}, bf16[4,3,32,1024]{3,2,1,0:T(8,128)(2,1)S(1)}, u32[]{:S(2)}, u32[]{:S(2)}) %collective-permute-start.3) | collective-permute-done | bytes 786464 | tf_op jit(solution)/shard_map/ppermute | solution.py:34
  201.6 1.9 pad_maximum_fusion.2
  203.4 2.6 gather_fusion.1
  206.1 2.2 bitcast_select_fusion
  208.3 4.9 %collective-permute-start.6 = (bf16[16,3,32,1024]{3,2,1,0:T(8,128)(2,1)}, bf16[16,3,32,1024]{3,2,1,0:T(8,128)(2,1)}, u32[]{:S(2)}, u32[]{:S(2)}) collective-permute-start(bf16[16,3,32,1024]{3,2,1,0:T(8,128)(2,1)} %bitcast_select_fusion), channel_id=1, source_target_pairs={{0,8},{8,0},{16,24},{24,16},{32,40},{40,32},{48,56},{56,48},{64,72... | collective-permute-start | bytes 9437192 | tf_op jit(solution)/shard_map/ppermute | solution.py:34
  213.2 1.8 broadcast_multiply_fusion.2
  215.4 4.6 %collective-permute-done.6 = bf16[16,3,32,1024]{3,2,1,0:T(8,128)(2,1)} collective-permute-done((bf16[16,3,32,1024]{3,2,1,0:T(8,128)(2,1)}, bf16[16,3,32,1024]{3,2,1,0:T(8,128)(2,1)}, u32[]{:S(2)}, u32[]{:S(2)}) %collective-permute-start.6) | collective-permute-done | bytes 3145760 | tf_op jit(solution)/shard_map/ppermute | solution.py:34
  219.9 3.4 fusion.3
  223.3 4.4 %gather_fusion.8 = bf16[2,16,3,32,512]{4,3,2,1,0:T(8,128)(2,1)} fusion(bf16[2,16,3,32,512]{4,3,2,1,0:T(8,128)(2,1)} %get-tuple-element.38, s32[1024]{0:T(1024)S(1)} %pad_clamp_fusion), kind=kCustom, calls=%fused_computation.8 | custom fusion | bytes 6291464 | tf_op jit(solution)/shard_map/jit(_take)/gather | solution.py:37
  227.7 2.4 gather_fusion.9
  230.1 3.9 pad_maximum_fusion
  234.1 4.0 copy.106
  238.0 1.5 fusion.23
  239.6 4.0 convolution_bitcast_fusion
  243.6 1.3 reshape.353
  245.0 8.2 %multiply_reduce_fusion = (f32[3]{0:T(128)S(1)}, f32[3,32,1024]{2,1,0:T(8,128)S(1)}) fusion(bf16[2,4,4,3,32,1024]{5,4,2,1,0,3:T(8,128)(2,1)} %bitcast.116, pred[2]{0:T(512)(128)(4,1)S(1)} %compare_and_fusion.2, f32[3,32,4,4,2,32]{5,4,3,2,1,0:T(2,128)S(1)} %reshape.353), kind=kOutput, calls=%fused_computation.51 | convolution fusion | flops 1211301888 | bytes 7077902 | tf_op jit(solution)/shard_map/smzxcr,cxzsrk->smk/dot_general | solution.py:90
  253.2 1.7 collective-permute-start.9
  254.9 1.3 collective-permute-start.8
  256.2 1.4 collective-permute-start.7
  257.6 3.6 collective-permute-done.8
  262.0 1.5 collective-permute-start.12
  263.5 2.2 collective-permute-start.11
  265.8 1.6 collective-permute-done.11
  267.5 1.8 collective-permute-done.10
  270.3 3.6 collective-permute-start.13
  273.8 0.8 collective-permute-done.13
  275.6 0.9 bitcast_subtract_fusion
  276.6 3.6 collective-permute-start.16
  280.2 3.7 collective-permute-start.15
  283.9 0.8 broadcast_multiply_fusion.1
  284.7 0.8 broadcast_multiply_fusion
  286.1 1.1 collective-permute-done.15
  287.4 0.6 gather_fusion.5
  288.5 1.1 collective-permute-start.17
  289.7 28.6 %all-gather.8.cloned.1.call-done = f32[24,32,1024]{2,1,0:T(8,128)} async-done(((f32[3,32,1024]{2,1,0:T(8,128)}), f32[24,32,1024]{2,1,0:T(8,128)}) %all-gather.8.cloned.1.call-update) | async-done | bytes 3145744 | tf_op jit(solution)/shard_map/all_gather | solution.py:104
  318.2 5.3 %fusion.4 = f32[1,32,1024]{2,0,1:T(1,128)S(1)} fusion(f32[24,32,1024]{2,1,0:T(8,128)} %all-gather.8.cloned.1.call-done, s32[]{:T(128)} %bitcast), kind=kOutput, calls=%fused_computation.21 | convolution fusion | flops 9437208 | bytes 3276804 | tf_op jit(solution)/shard_map/ji,irc->jrc/dot_general | solution.py:107
  323.6 0.7 copy.167
  324.7 0.8 gather_fusion.6
  325.7 3.4 collective-permute-start.20
  329.2 1.1 collective-permute-done.20
  331.2 0.7 divide_subtract_fusion
  331.8 2.0 copy.124
  333.8 5.0 %fusion.50 = f32[3,32,1024]{2,1,0:T(8,128)S(1)} fusion(bf16[3,32,1024]{2,1,0:T(8,128)(2,1)} %copy.105, bf16[3,1024,1024]{2,1,0:T(8,128)(2,1)} %all-gather.6.cloned.1.call-done), kind=kOutput, calls=%fused_computation.134 | convolution fusion | flops 201326592 | bytes 6881280 | tf_op jit(solution)/shard_map/src,snc->srn/dot_general | solution.py:77
  339.4 1.0 copy.122
  340.4 1.5 fusion.13
  342.4 1.0 copy.123
  343.4 43.9 %all-gather.10.cloned.1.call-done = f32[1024,1024]{1,0:T(8,128)} async-done(((f32[32,1024]{1,0:T(8,128)}), f32[1024,1024]{1,0:T(8,128)}) %all-gather.10.cloned.1.call-update) | async-done | bytes 4194320 | tf_op jit(solution)/shard_map/all_gather | solution.py:110
  387.3 4.8 %copy.169 = f32[1,1024,1024]{2,1,0:T(8,128)} copy(f32[1,1024,1024]{2,1,0:T(8,128)} %bitcast.117) | data formatting | bytes 8388608
  (108 shorter events, 9.6 us)
Async XLA Ops:
  7.2 232.4 %copy-start = (bf16[1,3,32,1024]{3,2,1,0:T(8,128)(2,1)S(1)}, bf16[1,3,32,1024]{3,2,1,0:T(8,128)(2,1)}, u32[]{:S(2)}) copy-start(bf16[1,3,32,1024]{3,2,1,0:T(8,128)(2,1)} %param.15) | copy-start | bytes 589828
  7.2 106.8 %reduce-scatter.2.cloned.1.call-start = ((), (), s32[]{:S(2)}) async-start(), calls=%async_computation.1 | async-start | bytes 4325376 | tf_op jit(solution)/shard_map/reduce_scatter | solution.py:68
  11.4 0.7 copy-start.13
  11.4 128.4 %copy-start.9 = (bf16[1,3,32,1024]{3,2,1,0:T(8,128)(2,1)S(1)}, bf16[1,3,32,1024]{3,2,1,0:T(8,128)(2,1)}, u32[]{:S(2)}) copy-start(bf16[1,3,32,1024]{3,2,1,0:T(8,128)(2,1)} %param.16) | copy-start | bytes 589828
  11.4 228.2 %all-gather.6.cloned.1.call-start = ((), (), s32[]{:S(2)}) async-start(), calls=%async_computation.2 | async-start | bytes 6488064 | tf_op jit(solution)/shard_map/all_gather | solution.py:76
  138.3 0.7 copy-start.1
  139.8 178.5 %all-gather.8.cloned.1.call-start = ((), (), s32[]{:S(2)}) async-start(), calls=%async_computation.3 | async-start | bytes 3538944 | tf_op jit(solution)/shard_map/all_gather | solution.py:104
  139.8 8.9 %collective-permute-start = (bf16[1,3,32,1024]{3,2,1,0:T(8,128)(2,1)S(1)}, bf16[1,3,32,1024]{3,2,1,0:T(8,128)(2,1)S(1)}, u32[]{:S(2)}, u32[]{:S(2)}) collective-permute-start(bf16[1,3,32,1024]{3,2,1,0:T(8,128)(2,1)S(1)} %copy-done.9), channel_id=1, source_target_pairs={{0,64},{8,72},{16,80},{24,88},{32,96},{40,104},{48,112},{56,120},{... | collective-permute-start | bytes 589832 | tf_op jit(solution)/shard_map/ppermute | solution.py:34
  141.6 8.8 %collective-permute-start.2 = (bf16[1,3,32,1024]{3,2,1,0:T(8,128)(2,1)S(1)}, bf16[1,3,32,1024]{3,2,1,0:T(8,128)(2,1)S(1)}, u32[]{:S(2)}, u32[]{:S(2)}) collective-permute-start(bf16[1,3,32,1024]{3,2,1,0:T(8,128)(2,1)S(1)} %copy-done.9), channel_id=1, source_target_pairs={{0,192},{8,200},{16,208},{24,216},{32,224},{40,232},{48,240},{56,2... | collective-permute-start | bytes 589832 | tf_op jit(solution)/shard_map/ppermute | solution.py:34
  143.5 11.8 %collective-permute-start.1 = (bf16[1,3,32,1024]{3,2,1,0:T(8,128)(2,1)S(1)}, bf16[1,3,32,1024]{3,2,1,0:T(8,128)(2,1)S(1)}, u32[]{:S(2)}, u32[]{:S(2)}) collective-permute-start(bf16[1,3,32,1024]{3,2,1,0:T(8,128)(2,1)S(1)} %copy-done.9), channel_id=1, source_target_pairs={{0,128},{8,136},{16,144},{24,152},{32,160},{40,168},{48,176},{56,1... | collective-permute-start | bytes 589832 | tf_op jit(solution)/shard_map/ppermute | solution.py:34
  157.0 13.8 %collective-permute-start.5 = (bf16[4,3,32,1024]{3,2,1,0:T(8,128)(2,1)}, bf16[4,3,32,1024]{3,2,1,0:T(8,128)(2,1)S(1)}, u32[]{:S(2)}, u32[]{:S(2)}) collective-permute-start(bf16[4,3,32,1024]{3,2,1,0:T(8,128)(2,1)} %broadcast_select_fusion), channel_id=1, source_target_pairs={{0,48},{8,56},{16,0},{24,8},{32,16},{40,24},{48,32},{56,40},{64,11... | collective-permute-start | bytes 2359304 | tf_op jit(solution)/shard_map/ppermute | solution.py:34
  157.0 14.3 %collective-permute-start.4 = (bf16[4,3,32,1024]{3,2,1,0:T(8,128)(2,1)}, bf16[4,3,32,1024]{3,2,1,0:T(8,128)(2,1)S(1)}, u32[]{:S(2)}, u32[]{:S(2)}) collective-permute-start(bf16[4,3,32,1024]{3,2,1,0:T(8,128)(2,1)} %broadcast_select_fusion), channel_id=1, source_target_pairs={{0,32},{8,40},{16,48},{24,56},{32,0},{40,8},{48,16},{56,24},{64,96... | collective-permute-start | bytes 2359304 | tf_op jit(solution)/shard_map/ppermute | solution.py:34
  157.0 44.6 %collective-permute-start.3 = (bf16[4,3,32,1024]{3,2,1,0:T(8,128)(2,1)}, bf16[4,3,32,1024]{3,2,1,0:T(8,128)(2,1)S(1)}, u32[]{:S(2)}, u32[]{:S(2)}) collective-permute-start(bf16[4,3,32,1024]{3,2,1,0:T(8,128)(2,1)} %broadcast_select_fusion), channel_id=1, source_target_pairs={{0,16},{8,24},{16,32},{24,40},{32,48},{40,56},{48,0},{56,8},{64,80... | collective-permute-start | bytes 2359304 | tf_op jit(solution)/shard_map/ppermute | solution.py:34
  208.3 11.7 %collective-permute-start.6 = (bf16[16,3,32,1024]{3,2,1,0:T(8,128)(2,1)}, bf16[16,3,32,1024]{3,2,1,0:T(8,128)(2,1)}, u32[]{:S(2)}, u32[]{:S(2)}) collective-permute-start(bf16[16,3,32,1024]{3,2,1,0:T(8,128)(2,1)} %bitcast_select_fusion), channel_id=1, source_target_pairs={{0,8},{8,0},{16,24},{24,16},{32,40},{40,32},{48,56},{56,48},{64,72... | collective-permute-start | bytes 9437192 | tf_op jit(solution)/shard_map/ppermute | solution.py:34
  234.0 4.0 %copy-start.2 = (bf16[3,32,1024]{2,0,1:T(4,128)(2,1)S(1)}, bf16[3,32,1024]{2,0,1:T(4,128)(2,1)}, u32[]{:S(2)}) copy-start(bf16[3,32,1024]{2,0,1:T(4,128)(2,1)} %copy-done.1) | copy-start | bytes 589828
  234.0 4.0 copy-start.5
  244.9 30.7 %copy-start.8 = (f32[1,3,32,1024]{3,2,1,0:T(8,128)S(1)}, f32[1,3,32,1024]{3,2,1,0:T(8,128)}, u32[]{:S(2)}) copy-start(f32[1,3,32,1024]{3,2,1,0:T(8,128)} %param.17) | copy-start | bytes 1179652
  244.9 31.6 %copy-start.12 = (bf16[1,8448]{1,0:T(2,128)(2,1)S(1)}, bf16[1,8448]{1,0:T(2,128)(2,1)}, u32[]{:S(2)}) copy-start(bf16[1,8448]{1,0:T(2,128)(2,1)} %param.19) | copy-start | bytes 50692
  244.9 39.0 %copy-start.6 = (f32[1,3,32,1024]{3,2,1,0:T(8,128)S(1)}, f32[1,3,32,1024]{3,2,1,0:T(8,128)}, u32[]{:S(2)}) copy-start(f32[1,3,32,1024]{3,2,1,0:T(8,128)} %param.13) | copy-start | bytes 1179652
  244.9 39.8 %copy-start.7 = (f32[1,3,32,1024]{3,2,1,0:T(8,128)S(1)}, f32[1,3,32,1024]{3,2,1,0:T(8,128)}, u32[]{:S(2)}) copy-start(f32[1,3,32,1024]{3,2,1,0:T(8,128)} %param.14) | copy-start | bytes 1179652
  253.2 4.4 %collective-permute-start.9 = (f32[1,2,3]{2,1,0:T(2,128)S(1)}, f32[1,2,3]{2,1,0:T(2,128)S(1)}, u32[]{:S(2)}, u32[]{:S(2)}) collective-permute-start(f32[1,2,3]{2,1,0:T(2,128)S(1)} %get-tuple-element.43), channel_id=1, source_target_pairs={{0,192},{8,200},{16,208},{24,216},{32,224},{40,232},{48,240},{56,2... | collective-permute-start | bytes 80 | tf_op jit(solution)/shard_map/ppermute | solution.py:34
  254.9 6.3 %collective-permute-start.8 = (f32[1,2,3]{2,1,0:T(2,128)S(1)}, f32[1,2,3]{2,1,0:T(2,128)S(1)}, u32[]{:S(2)}, u32[]{:S(2)}) collective-permute-start(f32[1,2,3]{2,1,0:T(2,128)S(1)} %get-tuple-element.43), channel_id=1, source_target_pairs={{0,128},{8,136},{16,144},{24,152},{32,160},{40,168},{48,176},{56,1... | collective-permute-start | bytes 80 | tf_op jit(solution)/shard_map/ppermute | solution.py:34
  256.2 5.1 %collective-permute-start.7 = (f32[1,2,3]{2,1,0:T(2,128)S(1)}, f32[1,2,3]{2,1,0:T(2,128)S(1)}, u32[]{:S(2)}, u32[]{:S(2)}) collective-permute-start(f32[1,2,3]{2,1,0:T(2,128)S(1)} %get-tuple-element.43), channel_id=1, source_target_pairs={{0,64},{8,72},{16,80},{24,88},{32,96},{40,104},{48,112},{56,120},{... | collective-permute-start | bytes 80 | tf_op jit(solution)/shard_map/ppermute | solution.py:34
  262.0 3.7 collective-permute-start.12
  263.5 4.0 collective-permute-start.11
  265.7 3.7 collective-permute-start.10
  270.3 4.4 %collective-permute-start.13 = (f32[16,2,3]{0,1,2:T(2,128)S(1)}, f32[16,2,3]{0,1,2:T(2,128)S(1)}, u32[]{:S(2)}, u32[]{:S(2)}) collective-permute-start(f32[16,2,3]{0,1,2:T(2,128)S(1)} %broadcast_select_fusion.5), channel_id=1, source_target_pairs={{0,8},{8,0},{16,24},{24,16},{32,40},{40,32},{48,56},{56,48},{64,72... | collective-permute-start | bytes 1160 | tf_op jit(solution)/shard_map/ppermute | solution.py:34
  276.5 110.8 %all-gather.10.cloned.1.call-start = ((), (), s32[]{:S(2)}) async-start(), calls=%async_computation.4 | async-start | bytes 4325376 | tf_op jit(solution)/shard_map/all_gather | solution.py:110
  276.5 9.6 %collective-permute-start.14 = (bf16[1,8448]{1,0:T(2,128)(2,1)S(1)}, bf16[1,8448]{1,0:T(2,128)(2,1)S(1)}, u32[]{:S(2)}, u32[]{:S(2)}) collective-permute-start(bf16[1,8448]{1,0:T(2,128)(2,1)S(1)} %copy-done.12), channel_id=1, source_target_pairs={{0,64},{8,72},{16,80},{24,88},{32,96},{40,104},{48,112},{56,120},{... | collective-permute-start | bytes 50696 | tf_op jit(solution)/shard_map/ppermute | solution.py:34
  276.6 9.5 %collective-permute-start.16 = (bf16[1,8448]{1,0:T(2,128)(2,1)S(1)}, bf16[1,8448]{1,0:T(2,128)(2,1)S(1)}, u32[]{:S(2)}, u32[]{:S(2)}) collective-permute-start(bf16[1,8448]{1,0:T(2,128)(2,1)S(1)} %copy-done.12), channel_id=1, source_target_pairs={{0,192},{8,200},{16,208},{24,216},{32,224},{40,232},{48,240},{56,2... | collective-permute-start | bytes 50696 | tf_op jit(solution)/shard_map/ppermute | solution.py:34
  280.2 7.0 %collective-permute-start.15 = (bf16[1,8448]{1,0:T(2,128)(2,1)S(1)}, bf16[1,8448]{1,0:T(2,128)(2,1)S(1)}, u32[]{:S(2)}, u32[]{:S(2)}) collective-permute-start(bf16[1,8448]{1,0:T(2,128)(2,1)S(1)} %copy-done.12), channel_id=1, source_target_pairs={{0,128},{8,136},{16,144},{24,152},{32,160},{40,168},{48,176},{56,1... | collective-permute-start | bytes 50696 | tf_op jit(solution)/shard_map/ppermute | solution.py:34
  288.1 36.2 %collective-permute-start.19 = (bf16[4,8448]{1,0:T(4,128)(2,1)S(1)}, bf16[4,8448]{1,0:T(4,128)(2,1)S(1)}, u32[]{:S(2)}, u32[]{:S(2)}) collective-permute-start(bf16[4,8448]{1,0:T(4,128)(2,1)S(1)} %broadcast_select_fusion.3), channel_id=1, source_target_pairs={{0,48},{8,56},{16,0},{24,8},{32,16},{40,24},{48,32},{56,40},{64,11... | collective-permute-start | bytes 202760 | tf_op jit(solution)/shard_map/ppermute | solution.py:34
  288.2 36.2 %collective-permute-start.18 = (bf16[4,8448]{1,0:T(4,128)(2,1)S(1)}, bf16[4,8448]{1,0:T(4,128)(2,1)S(1)}, u32[]{:S(2)}, u32[]{:S(2)}) collective-permute-start(bf16[4,8448]{1,0:T(4,128)(2,1)S(1)} %broadcast_select_fusion.3), channel_id=1, source_target_pairs={{0,32},{8,40},{16,48},{24,56},{32,0},{40,8},{48,16},{56,24},{64,96... | collective-permute-start | bytes 202760 | tf_op jit(solution)/shard_map/ppermute | solution.py:34
  288.5 35.9 %collective-permute-start.17 = (bf16[4,8448]{1,0:T(4,128)(2,1)S(1)}, bf16[4,8448]{1,0:T(4,128)(2,1)S(1)}, u32[]{:S(2)}, u32[]{:S(2)}) collective-permute-start(bf16[4,8448]{1,0:T(4,128)(2,1)S(1)} %broadcast_select_fusion.3), channel_id=1, source_target_pairs={{0,16},{8,24},{16,32},{24,40},{32,48},{40,56},{48,0},{56,8},{64,80... | collective-permute-start | bytes 202760 | tf_op jit(solution)/shard_map/ppermute | solution.py:34
  324.2 6.9 %copy-start.10 = (f32[8448]{0:T(1024)S(1)}, f32[8448]{0:T(1024)}, u32[]{:S(2)}) copy-start(f32[8448]{0:T(1024)} %param.20) | copy-start | bytes 101380
  324.2 6.9 %copy-start.11 = (f32[8448]{0:T(1024)S(1)}, f32[8448]{0:T(1024)}, u32[]{:S(2)}) copy-start(f32[8448]{0:T(1024)} %param.21) | copy-start | bytes 101380
  325.7 4.6 %collective-permute-start.20 = (bf16[16,8448]{1,0:T(8,128)(2,1)S(1)}, bf16[16,8448]{1,0:T(8,128)(2,1)S(1)}, u32[]{:S(2)}, u32[]{:S(2)}) collective-permute-start(bf16[16,8448]{1,0:T(8,128)(2,1)S(1)} %broadcast_select_fusion.1), channel_id=1, source_target_pairs={{0,8},{8,0},{16,24},{24,16},{32,40},{40,32},{48,56},{56,48},{64,72... | collective-permute-start | bytes 811016 | tf_op jit(solution)/shard_map/ppermute | solution.py:34
  330.3 10.1 %slice-start = ((s8[6291456]{0:T(1024)(128)(4,1)}), s8[2097152]{0:T(1024)(128)(4,1)S(1)}, s32[]{:S(2)}) async-start(s8[6291456]{0:T(1024)(128)(4,1)} %bitcast.113), calls=%async_computation.5 | async-start | bytes 4194304
  333.8 5.0 %copy-start.4 = (f32[1,3,32,1024]{3,2,1,0:T(8,128)S(1)}, f32[1,3,32,1024]{3,2,1,0:T(8,128)}, u32[]{:S(2)}) copy-start(f32[1,3,32,1024]{3,2,1,0:T(8,128)} %broadcast_multiply_fusion.1) | copy-start | bytes 1179652
  333.8 6.5 %slice-start.1 = ((s8[6291456]{0:T(1024)(128)(4,1)}), s8[4194304]{0:T(1024)(128)(4,1)S(1)}, s32[]{:S(2)}) async-start(s8[6291456]{0:T(1024)(128)(4,1)} %bitcast.113), calls=%async_computation.6 | async-start | bytes 8388608
  340.4 1.5 copy-start.3
Sparse Core Ops, SparseCore 0:
  12.5 101.4 reduce-scatter.1
  139.9 80.2 all-gather.5
  276.6 41.5 all-gather.7
  324.4 62.8 all-gather.9

commit v3 on v2

--- a/solution.py
+++ b/solution.py
@@ -38,6 +38,30 @@
     return bundle.reshape((2, 4, rep_count // 8) + value.shape)
 
 
+def own_gather(value, own_count):
+    own_here = lax.axis_index("own")
+    parts = [value]
+    for shift in range(1, own_count):
+        pairs = [(j, (j + shift) % own_count) for j in range(own_count)]
+        parts.append(lax.ppermute(value, "own", pairs))
+    stacked = jnp.stack(parts)
+    order = (own_here - jnp.arange(own_count, dtype=jnp.int32)) % own_count
+    return jnp.take(stacked, order, axis=0)
+
+
+def own_route(slots, owners, slot_index, own_count):
+    own_here = lax.axis_index("own")
+    parts = [lax.dynamic_index_in_dim(slots, slot_index[own_here], 0, keepdims=False)]
+    for shift in range(1, own_count):
+        pairs = [(j, (j + shift) % own_count) for j in range(own_count)]
+        dest = (own_here + shift) % own_count
+        chunk = lax.dynamic_index_in_dim(slots, slot_index[dest], 0, keepdims=False)
+        parts.append(lax.ppermute(chunk, "own", pairs))
+    stacked = jnp.stack(parts)
+    source_shift = (own_here - owners[own_here]) % own_count
+    return lax.dynamic_index_in_dim(stacked, source_shift, 0, keepdims=True)
+
+
 def shards(
     grads,
     owners,
@@ -67,7 +91,8 @@
     grad_rows = grads[0, 0].astype(jnp.float32).reshape(rep_count, row_count, block_size)
     summed = lax.psum_scatter(grad_rows, "rep", scatter_dimension=0, tiled=False)
     grad_held = lax.optimization_barrier(summed).astype(jnp.bfloat16)[None]
-    shard_part = lax.all_gather(grad_held, "own", axis=0, tiled=True)
+    own_count = owners.shape[0] // blk_local
+    shard_part = own_gather(grad_held[0], own_count)
     wanted = (owners[None, :] == own_here) & (slot_index[None, :] == slot_range[:, None])
     owned_grad = jnp.einsum(
         "ki,irc->krc", wanted.astype(jnp.bfloat16), shard_part, preferred_element_type=jnp.float32
@@ -100,13 +125,7 @@
     cell_count = float(block_size * block_size)
     graft_scale = jnp.sqrt(adam_total / cell_count) / jnp.sqrt(dir_total / cell_count + GRAFT_EPS)
     updated = slot_weights[0] - STEP_SIZE * graft_scale[:, None, None] * direction
-    mine_target = lax.dynamic_slice_in_dim(target, own_here * blk_local, blk_local)
-    shard_part = lax.all_gather(updated, "own", axis=0, tiled=True)
-    length = shard_part.shape[0]
-    wanted = mine_target[:, None] == jnp.arange(length, dtype=jnp.int32)[None, :]
-    held_rows = jnp.einsum(
-        "ji,irc->jrc", wanted.astype(jnp.float32), shard_part, precision=lax.Precision.HIGHEST
-    )
+    held_rows = own_route(updated, owners, slot_index, own_count)
     new_weights = lax.all_gather(held_rows, "rep", axis=1, tiled=True)
     new_left = STAT_DECAY * left_stats[0] + (1.0 - STAT_DECAY) / block_size * left_part
     new_right = STAT_DECAY * right_stats[0] + (1.0 - STAT_DECAY) / block_size * right_part

time: 399 us -> 421 us (1.055); the launches traced: 399 us -> 412 us
  starting transfers between devices: 37.9 us -> 70.4 us
  blocking collectives: 23 us -> 0 us
  between operations: 14.2 us -> 30.5 us
  waiting for transfers between devices: 240 us -> 229 us
  matrix products: 24.4 us -> 19.2 us
    ppermute x0 -> x14, waiting for transfers between devices: none -> 35.8 us  [the longest x7 26.2 us: own_route(): parts.append(lax.ppermute(chunk, 'own', pairs))]
    all_gather x1 -> x0, waiting for transfers between devices: 28.6 us -> none  [shards(): shard_part = lax.all_gather(updated, 'own', axis=0, tiled=True)]
    all_gather x1 -> x0, blocking collectives: 23 us -> none  [shards(): shard_part = lax.all_gather(grad_held, 'own', axis=0, tiled=True)]
    ppermute x21, starting transfers between devices: 37.8 us -> 58.1 us  [rep_gather(): parts.append(lax.ppermute(bundle, 'rep', pairs))]
    ppermute x21, waiting for transfers between devices: 65.5 us -> 50.5 us  [rep_gather(): parts.append(lax.ppermute(bundle, 'rep', pairs))]
    ppermute x0 -> x14, starting transfers between devices: none -> 12.1 us  [the longest x7 7.6 us: own_gather(): parts.append(lax.ppermute(value, 'own', pairs))]
    dot_general x1 -> x0, matrix products: 5.33 us -> none  [shards(): jnp.einsum('ji,irc->jrc', wanted.astype(jnp.float32), shard_part, precisi...]
    unnamed x37 -> x47, local copies, waits for them, and re-layouts: 14.1 us -> 14.8 us
  transfers between devices with their start and end apart: 25 -> 38, of which waited for: 16 -> 22; matrix products, arithmetic and copies ran while one was open for 14% -> 13% of each run, Pallas kernels for 0% -> 0%
where the time goes in v3:
time: 421 us; the launch traced here: 412 us
  waiting for transfers between devices  229 us (54%)
  starting transfers between devices  70.4 us (17%)
  local copies, waits for them, and re-layouts  34.1 us (8%)
  between operations  30.5 us (7%)
  other arithmetic  29.5 us (7%)
  matrix products  19.2 us (5%)
    reduce_scatter x1, waiting for transfers between devices, shards(): lax.psum_scatter(grad_rows, 'rep', scatter_dimension=0, tiled=False)  102 us
    ppermute x21, starting transfers between devices, rep_gather(): parts.append(lax.ppermute(bundle, 'rep', pairs))  58.1 us
    ppermute x21, waiting for transfers between devices, rep_gather(): parts.append(lax.ppermute(bundle, 'rep', pairs))  50.5 us
    all_gather x1, waiting for transfers between devices, shards(): new_weights = lax.all_gather(held_rows, 'rep', axis=1, tiled=True)  40.5 us
    ppermute x7, waiting for transfers between devices, own_route(): parts.append(lax.ppermute(chunk, 'own', pairs))  26.2 us
    unnamed x47, local copies, waits for them, and re-layouts  14.8 us
    gather x16, local copies, waits for them, and re-layouts, rep_gather(): jnp.take(stacked, order, axis=0)  14.1 us
    ppermute x7, waiting for transfers between devices, own_gather(): parts.append(lax.ppermute(value, 'own', pairs))  9.52 us
  transfers between devices with their start and end apart: 38, of which 22 were waited for; matrix products, arithmetic and copies ran while one was open for 13% of the time, Pallas kernels for 0%

profile of v3, /device:TPU:1, one launch (start us, length us, event | category | flops | bytes accessed | tf_op | source)
XLA Modules:
  0.0 412.2 jit_solution(2009257095593239812)
XLA Ops:
  7.2 4.1 %convert.1 = f32[32,32,1024]{2,1,0:T(8,128)} convert(bf16[32,32,1024]{2,1,0:T(8,128)(2,1)} %bitcast.163) | non-fusion elementwise | flops 1048576 | bytes 6291456 | tf_op jit(solution)/shard_map/convert_element_type | solution.py:91
  12.2 101.8 %reduce-scatter.2.cloned.1.call-done = f32[1,32,1024]{2,1,0:T(8,128)} async-done(((f32[32,32,1024]{2,1,0:T(8,128)}), f32[1,32,1024]{2,1,0:T(8,128)}) %reduce-scatter.2.cloned.1.call-update) | async-done | bytes 131088 | tf_op jit(solution)/shard_map/reduce_scatter | solution.py:92
  114.0 0.9 bitcast_dynamic-update-slice_fusion.14
  114.9 1.3 collective-permute-start
  116.2 2.3 collective-permute-start.5
  118.5 1.0 collective-permute-start.4
  119.5 0.9 collective-permute-start.3
  120.4 2.1 collective-permute-start.2
  122.5 6.2 %collective-permute-done.1 = bf16[32,1024]{1,0:T(8,128)(2,1)S(1)} collective-permute-done((bf16[32,1024]{1,0:T(8,128)(2,1)S(1)}, bf16[32,1024]{1,0:T(8,128)(2,1)S(1)}, u32[]{:S(2)}, u32[]{:S(2)}) %collective-permute-start.1) | collective-permute-done | bytes 65568 | tf_op jit(solution)/shard_map/ppermute | solution.py:46
  128.8 3.3 collective-permute-done.6
  134.8 1.4 collective-permute-start.7
  136.2 2.2 collective-permute-start.9
  138.5 3.4 collective-permute-start.8
  142.0 6.3 %collective-permute-done.9 = bf16[1,3,32,1024]{3,2,1,0:T(8,128)(2,1)S(1)} collective-permute-done((bf16[1,3,32,1024]{3,2,1,0:T(8,128)(2,1)S(1)}, bf16[1,3,32,1024]{3,2,1,0:T(8,128)(2,1)S(1)}, u32[]{:S(2)}, u32[]{:S(2)}) %collective-permute-start.9) | collective-permute-done | bytes 196640 | tf_op jit(solution)/shard_map/ppermute | solution.py:34
  148.3 5.8 %collective-permute-done.8 = bf16[1,3,32,1024]{3,2,1,0:T(8,128)(2,1)S(1)} collective-permute-done((bf16[1,3,32,1024]{3,2,1,0:T(8,128)(2,1)S(1)}, bf16[1,3,32,1024]{3,2,1,0:T(8,128)(2,1)S(1)}, u32[]{:S(2)}, u32[]{:S(2)}) %collective-permute-start.8) | collective-permute-done | bytes 196640 | tf_op jit(solution)/shard_map/ppermute | solution.py:34
  154.8 1.0 broadcast_select_fusion
  155.8 12.2 %collective-permute-start.10 = (bf16[4,3,32,1024]{3,2,1,0:T(8,128)(2,1)}, bf16[4,3,32,1024]{3,2,1,0:T(8,128)(2,1)S(1)}, u32[]{:S(2)}, u32[]{:S(2)}) collective-permute-start(bf16[4,3,32,1024]{3,2,1,0:T(8,128)(2,1)} %broadcast_select_fusion), channel_id=1, source_target_pairs={{0,16},{8,24},{16,32},{24,40},{32,48},{40,56},{48,0},{56,8},{64,80... | collective-permute-start | bytes 2359304 | tf_op jit(solution)/shard_map/ppermute | solution.py:34
  168.4 3.1 collective-permute-done.12
  171.5 1.3 collective-permute-done.11
  172.8 25.0 %collective-permute-done.10 = bf16[4,3,32,1024]{3,2,1,0:T(8,128)(2,1)S(1)} collective-permute-done((bf16[4,3,32,1024]{3,2,1,0:T(8,128)(2,1)}, bf16[4,3,32,1024]{3,2,1,0:T(8,128)(2,1)S(1)}, u32[]{:S(2)}, u32[]{:S(2)}) %collective-permute-start.10) | collective-permute-done | bytes 786464 | tf_op jit(solution)/shard_map/ppermute | solution.py:34
  197.8 1.9 pad_maximum_fusion.2
  199.7 2.6 gather_fusion.2
  202.3 2.2 bitcast_select_fusion
  204.5 9.6 %collective-permute-start.13 = (bf16[16,3,32,1024]{3,2,1,0:T(8,128)(2,1)}, bf16[16,3,32,1024]{3,2,1,0:T(8,128)(2,1)}, u32[]{:S(2)}, u32[]{:S(2)}) collective-permute-start(bf16[16,3,32,1024]{3,2,1,0:T(8,128)(2,1)} %bitcast_select_fusion), channel_id=1, source_target_pairs={{0,8},{8,0},{16,24},{24,16},{32,40},{40,32},{48,56},{56,48},{64,72... | collective-permute-start | bytes 9437192 | tf_op jit(solution)/shard_map/ppermute | solution.py:34
  214.0 3.6 collective-permute-start.30
  217.6 5.1 %collective-permute-start.29 = (bf16[1,8448]{1,0:T(2,128)(2,1)S(1)}, bf16[1,8448]{1,0:T(2,128)(2,1)S(1)}, u32[]{:S(2)}, u32[]{:S(2)}) collective-permute-start(bf16[1,8448]{1,0:T(2,128)(2,1)S(1)} %copy-done.10), channel_id=1, source_target_pairs={{0,128},{8,136},{16,144},{24,152},{32,160},{40,168},{48,176},{56,1... | collective-permute-start | bytes 50696 | tf_op jit(solution)/shard_map/ppermute | solution.py:34
  222.8 1.8 broadcast_multiply_fusion.1
  224.6 1.8 broadcast_multiply_fusion
  226.3 1.8 broadcast_multiply_fusion.2
  245.8 0.9 maximum_bitcast_fusion.1
  247.7 3.4 fusion.3
  251.1 4.3 %gather_fusion.9 = bf16[2,16,3,32,512]{4,3,2,1,0:T(8,128)(2,1)} fusion(bf16[2,16,3,32,512]{4,3,2,1,0:T(8,128)(2,1)} %get-tuple-element.40, s32[1024]{0:T(1024)S(1)} %pad_clamp_fusion), kind=kCustom, calls=%fused_computation.9 | custom fusion | bytes 6291464 | tf_op jit(solution)/shard_map/jit(_take)/gather | solution.py:37
  255.4 2.4 gather_fusion.10
  257.8 3.9 pad_maximum_fusion
  261.8 4.0 copy.106
  265.8 1.5 fusion.21
  267.4 4.0 convolution_bitcast_fusion
  271.4 1.3 reshape.399
  272.7 8.2 %multiply_reduce_fusion = (f32[3]{0:T(128)S(1)}, f32[3,32,1024]{2,1,0:T(8,128)S(1)}) fusion(bf16[2,4,4,3,32,1024]{5,4,2,1,0,3:T(8,128)(2,1)} %bitcast.162, pred[2]{0:T(512)(128)(4,1)S(1)} %compare_and_fusion.3, f32[3,32,4,4,2,32]{5,4,3,2,1,0:T(2,128)S(1)} %reshape.399), kind=kOutput, calls=%fused_computation.51 | convolution fusion | flops 1211301888 | bytes 7077902 | tf_op jit(solution)/shard_map/smzxcr,cxzsrk->smk/dot_general | solution.py:115
  281.0 2.1 collective-permute-start.15
  284.3 3.1 collective-permute-done.15
  288.4 2.7 collective-permute-start.19
  291.0 0.9 collective-permute-start.17
  292.0 3.0 collective-permute-done.18
  296.0 3.9 collective-permute-start.20
  299.8 0.8 collective-permute-done.20
  302.3 1.5 collective-permute-start.32
  303.9 0.8 collective-permute-start.31
  304.6 3.6 collective-permute-start.27
  308.8 6.2 %collective-permute-done.22 = f32[32,1024]{1,0:T(8,128)S(1)} collective-permute-done((f32[32,1024]{1,0:T(8,128)S(1)}, f32[32,1024]{1,0:T(8,128)S(1)}, u32[]{:S(2)}, u32[]{:S(2)}) %collective-permute-start.22) | collective-permute-done | bytes 131104 | tf_op jit(solution)/shard_map/ppermute | solution.py:59
  315.0 4.7 %collective-permute-done.23 = f32[32,1024]{1,0:T(8,128)S(1)} collective-permute-done((f32[32,1024]{1,0:T(8,128)S(1)}, f32[32,1024]{1,0:T(8,128)S(1)}, u32[]{:S(2)}, u32[]{:S(2)}) %collective-permute-start.23) | collective-permute-done | bytes 131104 | tf_op jit(solution)/shard_map/ppermute | solution.py:59
  320.0 3.6 collective-permute-done.24
  324.2 4.4 %collective-permute-done.25 = f32[32,1024]{1,0:T(8,128)S(1)} collective-permute-done((f32[32,1024]{1,0:T(8,128)S(1)}, f32[32,1024]{1,0:T(8,128)S(1)}, u32[]{:S(2)}, u32[]{:S(2)}) %collective-permute-start.25) | collective-permute-done | bytes 131104 | tf_op jit(solution)/shard_map/ppermute | solution.py:59
  328.7 6.7 %collective-permute-done.26 = f32[32,1024]{1,0:T(8,128)S(1)} collective-permute-done((f32[32,1024]{1,0:T(8,128)S(1)}, f32[32,1024]{1,0:T(8,128)S(1)}, u32[]{:S(2)}, u32[]{:S(2)}) %collective-permute-start.26) | collective-permute-done | bytes 131104 | tf_op jit(solution)/shard_map/ppermute | solution.py:59
  336.5 0.8 gather_fusion.7
  337.5 8.0 %collective-permute-start.34 = (bf16[16,8448]{1,0:T(8,128)(2,1)S(1)}, bf16[16,8448]{1,0:T(8,128)(2,1)S(1)}, u32[]{:S(2)}, u32[]{:S(2)}) collective-permute-start(bf16[16,8448]{1,0:T(8,128)(2,1)S(1)} %broadcast_select_fusion.2), channel_id=1, source_target_pairs={{0,8},{8,0},{16,24},{24,16},{32,40},{40,32},{48,56},{56,48},{64,72... | collective-permute-start | bytes 811016 | tf_op jit(solution)/shard_map/ppermute | solution.py:34
  345.6 1.1 collective-permute-done.34
  348.2 2.0 copy.124
  350.2 5.1 %fusion.48 = f32[3,32,1024]{2,1,0:T(8,128)S(1)} fusion(bf16[3,32,1024]{2,1,0:T(8,128)(2,1)} %copy.105, bf16[3,1024,1024]{2,1,0:T(8,128)(2,1)} %all-gather.3.cloned.1.call-done), kind=kOutput, calls=%fused_computation.166 | convolution fusion | flops 201326592 | bytes 6881280 | tf_op jit(solution)/shard_map/src,snc->srn/dot_general | solution.py:102
  355.9 1.0 copy.122
  356.9 1.5 fusion.11
  359.0 1.0 copy.123
  359.9 40.5 %all-gather.5.cloned.1.call-done = f32[1,1024,1024]{2,1,0:T(8,128)} async-done(((f32[1,32,1024]{2,1,0:T(8,128)}), f32[1,1024,1024]{2,1,0:T(8,128)}) %all-gather.5.cloned.1.call-update) | async-done | bytes 4194320 | tf_op jit(solution)/shard_map/all_gather | solution.py:129
  400.4 4.8 %copy.177 = f32[1,1024,1024]{2,1,0:T(8,128)} copy(f32[1,1024,1024]{2,1,0:T(8,128)} %all-gather.5.cloned.1.call-done) | data formatting | bytes 8388608
  (148 shorter events, 18.2 us)
Async XLA Ops:
  7.2 260.2 %copy-start = (bf16[1,3,32,1024]{3,2,1,0:T(8,128)(2,1)S(1)}, bf16[1,3,32,1024]{3,2,1,0:T(8,128)(2,1)}, u32[]{:S(2)}) copy-start(bf16[1,3,32,1024]{3,2,1,0:T(8,128)(2,1)} %param.15) | copy-start | bytes 589828
  7.2 106.8 %reduce-scatter.2.cloned.1.call-start = ((), (), s32[]{:S(2)}) async-start(), calls=%async_computation.1 | async-start | bytes 4325376 | tf_op jit(solution)/shard_map/reduce_scatter | solution.py:92
  11.4 0.7 copy-start.12
  11.4 123.4 %copy-start.7 = (bf16[1,3,32,1024]{3,2,1,0:T(8,128)(2,1)S(1)}, bf16[1,3,32,1024]{3,2,1,0:T(8,128)(2,1)}, u32[]{:S(2)}) copy-start(bf16[1,3,32,1024]{3,2,1,0:T(8,128)(2,1)} %param.16) | copy-start | bytes 589828
  11.4 256.0 %all-gather.3.cloned.1.call-start = ((), (), s32[]{:S(2)}) async-start(), calls=%async_computation.2 | async-start | bytes 6488064 | tf_op jit(solution)/shard_map/all_gather | solution.py:101
  114.9 7.6 %collective-permute-start = (bf16[32,1024]{1,0:T(8,128)(2,1)S(1)}, bf16[32,1024]{1,0:T(8,128)(2,1)S(1)}, u32[]{:S(2)}, u32[]{:S(2)}) collective-permute-start(bf16[32,1024]{1,0:T(8,128)(2,1)S(1)} %get-tuple-element.39), channel_id=1, source_target_pairs={{0,1},{1,2},{2,3},{3,4},{4,5},{5,6},{6,7},{7,0},{8,9},{9,10},{10,1... | collective-permute-start | bytes 196616 | tf_op jit(solution)/shard_map/ppermute | solution.py:46
  116.2 12.6 %collective-permute-start.5 = (bf16[32,1024]{1,0:T(8,128)(2,1)S(1)}, bf16[32,1024]{1,0:T(8,128)(2,1)S(1)}, u32[]{:S(2)}, u32[]{:S(2)}) collective-permute-start(bf16[32,1024]{1,0:T(8,128)(2,1)S(1)} %get-tuple-element.39), channel_id=1, source_target_pairs={{0,6},{1,7},{2,0},{3,1},{4,2},{5,3},{6,4},{7,5},{8,14},{9,15},{10,... | collective-permute-start | bytes 196616 | tf_op jit(solution)/shard_map/ppermute | solution.py:46
  118.5 10.3 %collective-permute-start.4 = (bf16[32,1024]{1,0:T(8,128)(2,1)S(1)}, bf16[32,1024]{1,0:T(8,128)(2,1)S(1)}, u32[]{:S(2)}, u32[]{:S(2)}) collective-permute-start(bf16[32,1024]{1,0:T(8,128)(2,1)S(1)} %get-tuple-element.39), channel_id=1, source_target_pairs={{0,5},{1,6},{2,7},{3,0},{4,1},{5,2},{6,3},{7,4},{8,13},{9,14},{10,... | collective-permute-start | bytes 196616 | tf_op jit(solution)/shard_map/ppermute | solution.py:46
  119.5 9.3 %collective-permute-start.3 = (bf16[32,1024]{1,0:T(8,128)(2,1)S(1)}, bf16[32,1024]{1,0:T(8,128)(2,1)S(1)}, u32[]{:S(2)}, u32[]{:S(2)}) collective-permute-start(bf16[32,1024]{1,0:T(8,128)(2,1)S(1)} %get-tuple-element.39), channel_id=1, source_target_pairs={{0,4},{1,5},{2,6},{3,7},{4,0},{5,1},{6,2},{7,3},{8,12},{9,13},{10,... | collective-permute-start | bytes 196616 | tf_op jit(solution)/shard_map/ppermute | solution.py:46
  120.4 8.3 %collective-permute-start.2 = (bf16[32,1024]{1,0:T(8,128)(2,1)S(1)}, bf16[32,1024]{1,0:T(8,128)(2,1)S(1)}, u32[]{:S(2)}, u32[]{:S(2)}) collective-permute-start(bf16[32,1024]{1,0:T(8,128)(2,1)S(1)} %get-tuple-element.39), channel_id=1, source_target_pairs={{0,3},{1,4},{2,5},{3,6},{4,7},{5,0},{6,1},{7,2},{8,11},{9,12},{10,... | collective-permute-start | bytes 196616 | tf_op jit(solution)/shard_map/ppermute | solution.py:46
  122.5 6.2 %collective-permute-start.1 = (bf16[32,1024]{1,0:T(8,128)(2,1)S(1)}, bf16[32,1024]{1,0:T(8,128)(2,1)S(1)}, u32[]{:S(2)}, u32[]{:S(2)}) collective-permute-start(bf16[32,1024]{1,0:T(8,128)(2,1)S(1)} %get-tuple-element.39), channel_id=1, source_target_pairs={{0,2},{1,3},{2,4},{3,5},{4,6},{5,7},{6,0},{7,1},{8,10},{9,11},{10,... | collective-permute-start | bytes 196616 | tf_op jit(solution)/shard_map/ppermute | solution.py:46
  128.7 3.4 collective-permute-start.6
  133.3 0.7 copy-start.1
  134.8 265.7 %all-gather.5.cloned.1.call-start = ((), (), s32[]{:S(2)}) async-start(), calls=%async_computation.3 | async-start | bytes 4325376 | tf_op jit(solution)/shard_map/all_gather | solution.py:129
  134.8 7.2 %collective-permute-start.7 = (bf16[1,3,32,1024]{3,2,1,0:T(8,128)(2,1)S(1)}, bf16[1,3,32,1024]{3,2,1,0:T(8,128)(2,1)S(1)}, u32[]{:S(2)}, u32[]{:S(2)}) collective-permute-start(bf16[1,3,32,1024]{3,2,1,0:T(8,128)(2,1)S(1)} %copy-done.7), channel_id=1, source_target_pairs={{0,64},{8,72},{16,80},{24,88},{32,96},{40,104},{48,112},{56,120},{... | collective-permute-start | bytes 589832 | tf_op jit(solution)/shard_map/ppermute | solution.py:34
  136.2 12.1 %collective-permute-start.9 = (bf16[1,3,32,1024]{3,2,1,0:T(8,128)(2,1)S(1)}, bf16[1,3,32,1024]{3,2,1,0:T(8,128)(2,1)S(1)}, u32[]{:S(2)}, u32[]{:S(2)}) collective-permute-start(bf16[1,3,32,1024]{3,2,1,0:T(8,128)(2,1)S(1)} %copy-done.7), channel_id=1, source_target_pairs={{0,192},{8,200},{16,208},{24,216},{32,224},{40,232},{48,240},{56,2... | collective-permute-start | bytes 589832 | tf_op jit(solution)/shard_map/ppermute | solution.py:34
  138.5 15.6 %collective-permute-start.8 = (bf16[1,3,32,1024]{3,2,1,0:T(8,128)(2,1)S(1)}, bf16[1,3,32,1024]{3,2,1,0:T(8,128)(2,1)S(1)}, u32[]{:S(2)}, u32[]{:S(2)}) collective-permute-start(bf16[1,3,32,1024]{3,2,1,0:T(8,128)(2,1)S(1)} %copy-done.7), channel_id=1, source_target_pairs={{0,128},{8,136},{16,144},{24,152},{32,160},{40,168},{48,176},{56,1... | collective-permute-start | bytes 589832 | tf_op jit(solution)/shard_map/ppermute | solution.py:34
  155.8 15.7 %collective-permute-start.12 = (bf16[4,3,32,1024]{3,2,1,0:T(8,128)(2,1)}, bf16[4,3,32,1024]{3,2,1,0:T(8,128)(2,1)S(1)}, u32[]{:S(2)}, u32[]{:S(2)}) collective-permute-start(bf16[4,3,32,1024]{3,2,1,0:T(8,128)(2,1)} %broadcast_select_fusion), channel_id=1, source_target_pairs={{0,48},{8,56},{16,0},{24,8},{32,16},{40,24},{48,32},{56,40},{64,11... | collective-permute-start | bytes 2359304 | tf_op jit(solution)/shard_map/ppermute | solution.py:34
  155.8 17.0 %collective-permute-start.11 = (bf16[4,3,32,1024]{3,2,1,0:T(8,128)(2,1)}, bf16[4,3,32,1024]{3,2,1,0:T(8,128)(2,1)S(1)}, u32[]{:S(2)}, u32[]{:S(2)}) collective-permute-start(bf16[4,3,32,1024]{3,2,1,0:T(8,128)(2,1)} %broadcast_select_fusion), channel_id=1, source_target_pairs={{0,32},{8,40},{16,48},{24,56},{32,0},{40,8},{48,16},{56,24},{64,96... | collective-permute-start | bytes 2359304 | tf_op jit(solution)/shard_map/ppermute | solution.py:34
  155.8 42.0 %collective-permute-start.10 = (bf16[4,3,32,1024]{3,2,1,0:T(8,128)(2,1)}, bf16[4,3,32,1024]{3,2,1,0:T(8,128)(2,1)S(1)}, u32[]{:S(2)}, u32[]{:S(2)}) collective-permute-start(bf16[4,3,32,1024]{3,2,1,0:T(8,128)(2,1)} %broadcast_select_fusion), channel_id=1, source_target_pairs={{0,16},{8,24},{16,32},{24,40},{32,48},{40,56},{48,0},{56,8},{64,80... | collective-permute-start | bytes 2359304 | tf_op jit(solution)/shard_map/ppermute | solution.py:34
  202.3 11.7 %copy-start.10 = (bf16[1,8448]{1,0:T(2,128)(2,1)S(1)}, bf16[1,8448]{1,0:T(2,128)(2,1)}, u32[]{:S(2)}) copy-start(bf16[1,8448]{1,0:T(2,128)(2,1)} %param.19) | copy-start | bytes 50692
  204.5 43.2 %collective-permute-start.13 = (bf16[16,3,32,1024]{3,2,1,0:T(8,128)(2,1)}, bf16[16,3,32,1024]{3,2,1,0:T(8,128)(2,1)}, u32[]{:S(2)}, u32[]{:S(2)}) collective-permute-start(bf16[16,3,32,1024]{3,2,1,0:T(8,128)(2,1)} %bitcast_select_fusion), channel_id=1, source_target_pairs={{0,8},{8,0},{16,24},{24,16},{32,40},{40,32},{48,56},{56,48},{64,72... | collective-permute-start | bytes 9437192 | tf_op jit(solution)/shard_map/ppermute | solution.py:34
  214.0 31.1 %collective-permute-start.28 = (bf16[1,8448]{1,0:T(2,128)(2,1)S(1)}, bf16[1,8448]{1,0:T(2,128)(2,1)S(1)}, u32[]{:S(2)}, u32[]{:S(2)}) collective-permute-start(bf16[1,8448]{1,0:T(2,128)(2,1)S(1)} %copy-done.10), channel_id=1, source_target_pairs={{0,64},{8,72},{16,80},{24,88},{32,96},{40,104},{48,112},{56,120},{... | collective-permute-start | bytes 50696 | tf_op jit(solution)/shard_map/ppermute | solution.py:34
  214.0 31.1 %collective-permute-start.30 = (bf16[1,8448]{1,0:T(2,128)(2,1)S(1)}, bf16[1,8448]{1,0:T(2,128)(2,1)S(1)}, u32[]{:S(2)}, u32[]{:S(2)}) collective-permute-start(bf16[1,8448]{1,0:T(2,128)(2,1)S(1)} %copy-done.10), channel_id=1, source_target_pairs={{0,192},{8,200},{16,208},{24,216},{32,224},{40,232},{48,240},{56,2... | collective-permute-start | bytes 50696 | tf_op jit(solution)/shard_map/ppermute | solution.py:34
  217.6 27.5 %collective-permute-start.29 = (bf16[1,8448]{1,0:T(2,128)(2,1)S(1)}, bf16[1,8448]{1,0:T(2,128)(2,1)S(1)}, u32[]{:S(2)}, u32[]{:S(2)}) collective-permute-start(bf16[1,8448]{1,0:T(2,128)(2,1)S(1)} %copy-done.10), channel_id=1, source_target_pairs={{0,128},{8,136},{16,144},{24,152},{32,160},{40,168},{48,176},{56,1... | collective-permute-start | bytes 50696 | tf_op jit(solution)/shard_map/ppermute | solution.py:34
  245.2 0.6 copy-start.11
  261.8 4.0 copy-start.2
  261.8 4.0 copy-start.5
  272.7 28.9 %copy-start.6 = (f32[1,3,32,1024]{3,2,1,0:T(8,128)S(1)}, f32[1,3,32,1024]{3,2,1,0:T(8,128)}, u32[]{:S(2)}) copy-start(f32[1,3,32,1024]{3,2,1,0:T(8,128)} %param.17) | copy-start | bytes 1179652
  280.9 3.4 collective-permute-start.16
  281.0 6.4 %collective-permute-start.15 = (f32[1,2,3]{2,1,0:T(2,128)S(1)}, f32[1,2,3]{2,1,0:T(2,128)S(1)}, u32[]{:S(2)}, u32[]{:S(2)}) collective-permute-start(f32[1,2,3]{2,1,0:T(2,128)S(1)} %get-tuple-element.53), channel_id=1, source_target_pairs={{0,128},{8,136},{16,144},{24,152},{32,160},{40,168},{48,176},{56,1... | collective-permute-start | bytes 80 | tf_op jit(solution)/shard_map/ppermute | solution.py:34
  283.1 4.5 %collective-permute-start.14 = (f32[1,2,3]{2,1,0:T(2,128)S(1)}, f32[1,2,3]{2,1,0:T(2,128)S(1)}, u32[]{:S(2)}, u32[]{:S(2)}) collective-permute-start(f32[1,2,3]{2,1,0:T(2,128)S(1)} %get-tuple-element.53), channel_id=1, source_target_pairs={{0,64},{8,72},{16,80},{24,88},{32,96},{40,104},{48,112},{56,120},{... | collective-permute-start | bytes 80 | tf_op jit(solution)/shard_map/ppermute | solution.py:34
  288.4 3.5 collective-permute-start.19
  291.0 4.0 collective-permute-start.18
  291.0 4.1 collective-permute-start.17
  296.0 4.7 %collective-permute-start.20 = (f32[16,2,3]{0,1,2:T(2,128)S(1)}, f32[16,2,3]{0,1,2:T(2,128)S(1)}, u32[]{:S(2)}, u32[]{:S(2)}) collective-permute-start(f32[16,2,3]{0,1,2:T(2,128)S(1)} %broadcast_select_fusion.6), channel_id=1, source_target_pairs={{0,8},{8,0},{16,24},{24,16},{32,40},{40,32},{48,56},{56,48},{64,72... | collective-permute-start | bytes 1160 | tf_op jit(solution)/shard_map/ppermute | solution.py:34
  301.8 6.9 %collective-permute-start.21 = (f32[32,1024]{1,0:T(8,128)S(1)}, f32[32,1024]{1,0:T(8,128)S(1)}, u32[]{:S(2)}, u32[]{:S(2)}) collective-permute-start(f32[32,1024]{1,0:T(8,128)S(1)} %get-tuple-element.50), channel_id=1, source_target_pairs={{0,1},{1,2},{2,3},{3,4},{4,5},{5,6},{6,7},{7,0},{8,9},{9,10},{10,1... | collective-permute-start | bytes 393224 | tf_op jit(solution)/shard_map/ppermute | solution.py:59
  302.0 34.2 %collective-permute-start.33 = (bf16[4,8448]{1,0:T(4,128)(2,1)S(1)}, bf16[4,8448]{1,0:T(4,128)(2,1)S(1)}, u32[]{:S(2)}, u32[]{:S(2)}) collective-permute-start(bf16[4,8448]{1,0:T(4,128)(2,1)S(1)} %broadcast_select_fusion.4), channel_id=1, source_target_pairs={{0,48},{8,56},{16,0},{24,8},{32,16},{40,24},{48,32},{56,40},{64,11... | collective-permute-start | bytes 202760 | tf_op jit(solution)/shard_map/ppermute | solution.py:34
  302.3 33.9 %collective-permute-start.32 = (bf16[4,8448]{1,0:T(4,128)(2,1)S(1)}, bf16[4,8448]{1,0:T(4,128)(2,1)S(1)}, u32[]{:S(2)}, u32[]{:S(2)}) collective-permute-start(bf16[4,8448]{1,0:T(4,128)(2,1)S(1)} %broadcast_select_fusion.4), channel_id=1, source_target_pairs={{0,32},{8,40},{16,48},{24,56},{32,0},{40,8},{48,16},{56,24},{64,96... | collective-permute-start | bytes 202760 | tf_op jit(solution)/shard_map/ppermute | solution.py:34
  303.9 32.4 %collective-permute-start.31 = (bf16[4,8448]{1,0:T(4,128)(2,1)S(1)}, bf16[4,8448]{1,0:T(4,128)(2,1)S(1)}, u32[]{:S(2)}, u32[]{:S(2)}) collective-permute-start(bf16[4,8448]{1,0:T(4,128)(2,1)S(1)} %broadcast_select_fusion.4), channel_id=1, source_target_pairs={{0,16},{8,24},{16,32},{24,40},{32,48},{40,56},{48,0},{56,8},{64,80... | collective-permute-start | bytes 202760 | tf_op jit(solution)/shard_map/ppermute | solution.py:34
  304.6 30.8 %collective-permute-start.27 = (f32[32,1024]{1,0:T(8,128)S(1)}, f32[32,1024]{1,0:T(8,128)S(1)}, u32[]{:S(2)}, u32[]{:S(2)}) collective-permute-start(f32[32,1024]{1,0:T(8,128)S(1)} %get-tuple-element.44), channel_id=1, source_target_pairs={{0,7},{1,0},{2,1},{3,2},{4,3},{5,4},{6,5},{7,6},{8,15},{9,8},{10,9... | collective-permute-start | bytes 393224 | tf_op jit(solution)/shard_map/ppermute | solution.py:59
  308.7 6.2 %collective-permute-start.22 = (f32[32,1024]{1,0:T(8,128)S(1)}, f32[32,1024]{1,0:T(8,128)S(1)}, u32[]{:S(2)}, u32[]{:S(2)}) collective-permute-start(f32[32,1024]{1,0:T(8,128)S(1)} %get-tuple-element.49), channel_id=1, source_target_pairs={{0,2},{1,3},{2,4},{3,5},{4,6},{5,7},{6,0},{7,1},{8,10},{9,11},{10,... | collective-permute-start | bytes 393224 | tf_op jit(solution)/shard_map/ppermute | solution.py:59
  315.0 4.7 %collective-permute-start.23 = (f32[32,1024]{1,0:T(8,128)S(1)}, f32[32,1024]{1,0:T(8,128)S(1)}, u32[]{:S(2)}, u32[]{:S(2)}) collective-permute-start(f32[32,1024]{1,0:T(8,128)S(1)} %get-tuple-element.48), channel_id=1, source_target_pairs={{0,3},{1,4},{2,5},{3,6},{4,7},{5,0},{6,1},{7,2},{8,11},{9,12},{10,... | collective-permute-start | bytes 393224 | tf_op jit(solution)/shard_map/ppermute | solution.py:59
  319.7 3.9 collective-permute-start.24
  323.6 5.0 %collective-permute-start.25 = (f32[32,1024]{1,0:T(8,128)S(1)}, f32[32,1024]{1,0:T(8,128)S(1)}, u32[]{:S(2)}, u32[]{:S(2)}) collective-permute-start(f32[32,1024]{1,0:T(8,128)S(1)} %get-tuple-element.46), channel_id=1, source_target_pairs={{0,5},{1,6},{2,7},{3,0},{4,1},{5,2},{6,3},{7,4},{8,13},{9,14},{10,... | collective-permute-start | bytes 393224 | tf_op jit(solution)/shard_map/ppermute | solution.py:59
  328.6 6.7 %collective-permute-start.26 = (f32[32,1024]{1,0:T(8,128)S(1)}, f32[32,1024]{1,0:T(8,128)S(1)}, u32[]{:S(2)}, u32[]{:S(2)}) collective-permute-start(f32[32,1024]{1,0:T(8,128)S(1)} %get-tuple-element.45), channel_id=1, source_target_pairs={{0,6},{1,7},{2,0},{3,1},{4,2},{5,3},{6,4},{7,5},{8,14},{9,15},{10,... | collective-permute-start | bytes 393224 | tf_op jit(solution)/shard_map/ppermute | solution.py:59
  336.1 11.5 %copy-start.8 = (f32[8448]{0:T(1024)S(1)}, f32[8448]{0:T(1024)}, u32[]{:S(2)}) copy-start(f32[8448]{0:T(1024)} %param.20) | copy-start | bytes 101380
  336.1 11.5 %copy-start.9 = (f32[8448]{0:T(1024)S(1)}, f32[8448]{0:T(1024)}, u32[]{:S(2)}) copy-start(f32[8448]{0:T(1024)} %param.21) | copy-start | bytes 101380
  337.5 9.1 %collective-permute-start.34 = (bf16[16,8448]{1,0:T(8,128)(2,1)S(1)}, bf16[16,8448]{1,0:T(8,128)(2,1)S(1)}, u32[]{:S(2)}, u32[]{:S(2)}) collective-permute-start(bf16[16,8448]{1,0:T(8,128)(2,1)S(1)} %broadcast_select_fusion.2), channel_id=1, source_target_pairs={{0,8},{8,0},{16,24},{24,16},{32,40},{40,32},{48,56},{56,48},{64,72... | collective-permute-start | bytes 811016 | tf_op jit(solution)/shard_map/ppermute | solution.py:34
  346.7 10.2 %slice-start = ((s8[6291456]{0:T(1024)(128)(4,1)}), s8[2097152]{0:T(1024)(128)(4,1)S(1)}, s32[]{:S(2)}) async-start(s8[6291456]{0:T(1024)(128)(4,1)} %bitcast.159), calls=%async_computation.4 | async-start | bytes 4194304
  350.2 5.1 %copy-start.4 = (f32[1,3,32,1024]{3,2,1,0:T(8,128)S(1)}, f32[1,3,32,1024]{3,2,1,0:T(8,128)}, u32[]{:S(2)}) copy-start(f32[1,3,32,1024]{3,2,1,0:T(8,128)} %broadcast_multiply_fusion.1) | copy-start | bytes 1179652
  350.2 6.6 %slice-start.1 = ((s8[6291456]{0:T(1024)(128)(4,1)}), s8[4194304]{0:T(1024)(128)(4,1)S(1)}, s32[]{:S(2)}) async-start(s8[6291456]{0:T(1024)(128)(4,1)} %bitcast.159), calls=%async_computation.5 | async-start | bytes 8388608
  356.9 1.5 copy-start.3
Sparse Core Ops, SparseCore 0:
  12.5 101.4 reduce-scatter.1
  134.9 80.3 all-gather.2
  336.2 64.1 all-gather.4
